TPU v7x, 256 devices: a whole 4x4x8 slice. The times are simulated.
256 devices in a mesh: dp: 8 (over z_lo, core), expert: 32 (over x, z_hi, y).
Axes of the slice: x: 4, y: 4, z: 8 (z_hi: 2, z_lo: 4; z = z_hi * 4 + z_lo), core: 2. Of those that a mesh axis runs over, the one named last changes fastest.
Arguments:
- tokens: bfloat16 [16384, 2048], P(('dp', 'expert')), may hold values from -6 to 6
- routes: int32 [16384, 8], P(('dp', 'expert')), may hold values from 0 to 63, all different within a row; in each aligned block of 64 rows (0 to 63, 64 to 127, ...) at most 12 rows name the same one
- route_weight: int32 [16384, 8], P(('dp', 'expert')), may hold values from 1 to 65535
- capacity: int32 [64], replicated, may hold values from 8 to 10
- hot_expert: int32 [1], replicated, may hold values from 0 to 63
- w_gate: bfloat16 [64, 2048, 768], P('expert', 'dp'), may hold values from -0.125 to 0.125
- w_up: bfloat16 [64, 2048, 768], P('expert', 'dp'), may hold values from -0.125 to 0.125
- w_down: bfloat16 [64, 768, 2048], P('expert', None, 'dp'), may hold values from -0.21875 to 0.21875
Outputs:
- mixed: bfloat16 [16384, 2048], P(('dp', 'expert'))
All inputs are finite; a program needn't handle non-finite values.
Results may differ from a plain program's by a relative error of at most 0.0057.
Values may be sent and summed in bfloat16 or wider, within the bound.
No kernel may reach another device: no remote copies, remote signals or barrier semaphores. Data moves between devices by JAX's collectives and lax.ppermute only.
A program may use at most 128 MiB of HBM per device.

v0:
```python
import jax
import jax.numpy as jnp
from jax import lax
from jax.sharding import PartitionSpec as P

CAP = 10
MOST = 12


def per_device(tokens, routes, route_weight, capacity, hot_expert, w_gate, w_up, w_down):
    tok_rows = tokens.shape[0]
    width = tokens.shape[1]
    n_peer = lax.axis_size("expert")
    my_index = lax.axis_index("expert")
    exp_dev = w_gate.shape[0]
    experts = exp_dev * n_peer
    flat_e = routes.reshape(-1)
    weights = route_weight.astype(jnp.float32)
    share = (weights / jnp.sum(weights, axis=1, keepdims=True)).reshape(-1)
    onehot = (flat_e[:, None] == jnp.arange(experts, dtype=jnp.int32)[None, :]).astype(jnp.int32)
    before = jnp.cumsum(onehot, axis=0) - onehot
    rank = jnp.sum(onehot * before, axis=1)
    cap_of = jnp.sum(onehot * capacity[None, :], axis=1)
    hot = hot_expert[0]
    owner = hot // exp_dev
    hot_local = jnp.clip(hot - my_index * exp_dev, 0, exp_dev - 1)
    is_hot = flat_e == hot
    kept_cap = jnp.logical_and(jnp.logical_not(is_hot), rank < cap_of)
    target_cap = jnp.where(kept_cap, flat_e * CAP + rank, -1).reshape(tok_rows, -1)
    target_hot = jnp.where(is_hot, rank, -1).reshape(tok_rows, -1)
    select_cap = jnp.any(
        target_cap[None, :, :] == jnp.arange(experts * CAP, dtype=jnp.int32)[:, None, None], axis=2
    ).astype(jnp.bfloat16)
    select_hot = jnp.any(
        target_hot[None, :, :] == jnp.arange(MOST, dtype=jnp.int32)[:, None, None], axis=2
    ).astype(jnp.bfloat16)
    send_cap = jnp.dot(select_cap, tokens, preferred_element_type=jnp.float32).astype(jnp.bfloat16)
    send_cap = send_cap.reshape(n_peer, exp_dev * CAP, width)
    hot_rows = jnp.dot(select_hot, tokens, preferred_element_type=jnp.float32).astype(jnp.bfloat16)
    cap_slots = exp_dev * CAP
    owner_mask = (jnp.arange(n_peer, dtype=jnp.int32) == owner)[:, None, None]
    send_hot = jnp.where(owner_mask, hot_rows[None, :, :], jnp.zeros((), jnp.bfloat16))
    received = lax.all_to_all(
        jnp.concatenate([send_cap, send_hot], axis=1),
        "expert",
        split_axis=0,
        concat_axis=0,
        tiled=True,
    )
    recv_cap = received[:, :cap_slots].reshape(n_peer, exp_dev, CAP, width)
    recv_hot = received[:, cap_slots:]
    piece_gate = lax.all_gather(w_gate, "dp", axis=1, tiled=True)
    piece_up = lax.all_gather(w_up, "dp", axis=1, tiled=True)
    hot_gate = lax.dynamic_index_in_dim(piece_gate, hot_local, 0, keepdims=False)
    hot_up = lax.dynamic_index_in_dim(piece_up, hot_local, 0, keepdims=False)
    gate_cap = jnp.einsum(
        "pcrd,cdf->pcrf", recv_cap, piece_gate, preferred_element_type=jnp.float32
    )
    up_cap = jnp.einsum("pcrd,cdf->pcrf", recv_cap, piece_up, preferred_element_type=jnp.float32)
    gate_hot = jnp.einsum("prd,df->prf", recv_hot, hot_gate, preferred_element_type=jnp.float32)
    up_hot = jnp.einsum("prd,df->prf", recv_hot, hot_up, preferred_element_type=jnp.float32)
    gate_cap, up_cap, gate_hot, up_hot = (gate_cap, up_cap, gate_hot, up_hot)
    hidden_cap = (jax.nn.silu(gate_cap) * up_cap).astype(jnp.bfloat16)
    hidden_hot = (jax.nn.silu(gate_hot) * up_hot).astype(jnp.bfloat16)
    piece = lax.all_gather(w_down, "dp", axis=2, tiled=True)
    count = piece.shape[2]
    hot_down = lax.dynamic_index_in_dim(piece, hot_local, 0, keepdims=False)
    out_cap = jnp.einsum("pcrf,cfd->pcrd", hidden_cap, piece, preferred_element_type=jnp.float32)
    out_hot = jnp.einsum("prf,fd->prd", hidden_hot, hot_down, preferred_element_type=jnp.float32)
    out_cap = out_cap.reshape(n_peer, cap_slots, count)
    outgoing = jnp.concatenate([out_cap, out_hot], axis=1).astype(jnp.bfloat16)
    returned = lax.all_to_all(outgoing, "expert", split_axis=0, concat_axis=0, tiled=True)
    back_cap = returned[:, :cap_slots].reshape(experts * CAP, width)
    back_hot = lax.dynamic_index_in_dim(returned, owner, 0, keepdims=False)[cap_slots:]
    table = jnp.concatenate([back_cap, back_hot, jnp.zeros((1, width), jnp.bfloat16)], axis=0)
    where_row = jnp.where(
        kept_cap, flat_e * CAP + rank, jnp.where(is_hot, experts * CAP + rank, experts * CAP + MOST)
    )
    picked = jnp.take(table, where_row, axis=0)
    factor = jnp.where(jnp.logical_or(kept_cap, is_hot), share, 0.0)
    summed = jnp.sum(
        (picked.astype(jnp.float32) * factor[:, None]).reshape(tok_rows, -1, width), axis=1
    )
    return summed.astype(jnp.bfloat16)


def solution(mesh):
    in_specs = (
        P(("dp", "expert"), None),
        P(("dp", "expert"), None),
        P(("dp", "expert"), None),
        P(),
        P(),
        P("expert", "dp", None),
        P("expert", "dp", None),
        P("expert", None, "dp"),
    )
    out_specs = P(("dp", "expert"), None)
    return jax.shard_map(
        per_device, mesh=mesh, in_specs=in_specs, out_specs=out_specs, check_vma=False
    )
```

profile of v0, /device:TPU:37, one launch (start us, length us, event | category | flops | bytes accessed | tf_op | source)
XLA Modules:
  0.0 495.2 jit_solution(10126614187241409905)
XLA Ops:
  6.5 0.7 all-gather.4.cloned.1.call-update
  7.3 0.7 all-gather.6.cloned.1.call-update
  8.1 0.7 all-gather.8.cloned.1.call-update
  9.4 0.8 copy.35
  10.4 1.2 reduce-window.6
  11.6 0.2 slice_reduce_fusion
  12.3 0.5 fusion.35
  12.8 2.4 convolution_convert_fusion
  15.2 3.5 reshape.158
  19.1 2.7 pad_maximum_fusion
  21.8 13.0 %all-to-all-start = ((bf16[32,32,2048]{2,1,0:T(8,128)(2,1)}), bf16[32,32,2048]{2,1,0:T(8,128)(2,1)}, u32[]{:S(2)}, u32[]{:S(2)}) async-start(bf16[32,32,2048]{2,1,0:T(8,128)(2,1)} %pad_maximum_fusion), calls=%async_computation | async-start | bytes 8388608 | tf_op jit(solution)/shard_map/all_to_all | solution.py:43
  34.9 139.3 %all-to-all-done = bf16[32,32,2048]{2,1,0:T(8,128)(2,1)} async-done(((bf16[32,32,2048]{2,1,0:T(8,128)(2,1)}), bf16[32,32,2048]{2,1,0:T(8,128)(2,1)}, u32[]{:S(2)}, u32[]{:S(2)}) %all-to-all-start) | async-done | bytes 4194336 | tf_op jit(solution)/shard_map/all_to_all | solution.py:43
  174.1 2.3 slice.31
  176.5 1.4 copy.41
  177.9 3.6 slice.32
  181.5 6.3 %fusion.4 = f32[2,32,10,768]{3,1,2,0:T(8,128)} fusion(bf16[32,2,10,2048]{3,0,2,1:T(8,128)(2,1)S(1)} %bitcast.108, bf16[2,2048,768]{2,1,0:T(8,128)(2,1)} %all-gather.4.cloned.1.call-done), kind=kOutput, calls=%fused_computation.5 | convolution fusion | flops 2013265920 | bytes 10878976 | tf_op jit(solution)/shard_map/pcrd,cdf->pcrf/dot_general | solution.py:56
  187.9 61.1 %all-gather.6.cloned.1.call-done = bf16[2,2048,768]{2,1,0:T(8,128)(2,1)} async-done(((bf16[2,256,768]{2,1,0:T(8,128)(2,1)}), bf16[2,2048,768]{2,1,0:T(8,128)(2,1)}) %all-gather.6.cloned.1.call-update) | async-done | bytes 6291472 | tf_op jit(solution)/shard_map/all_gather | solution.py:53
  248.9 75.1 %all-gather.8.cloned.1.call-done = bf16[2,768,2048]{2,1,0:T(8,128)(2,1)} async-done(((bf16[2,768,256]{2,1,0:T(8,128)(2,1)}), bf16[2,768,2048]{2,1,0:T(8,128)(2,1)}) %all-gather.8.cloned.1.call-update) | async-done | bytes 6291472 | tf_op jit(solution)/shard_map/all_gather | solution.py:65
  324.0 11.0 %fusion.6 = bf16[2,32,10,2048]{3,1,2,0:T(8,128)(2,1)} fusion(bf16[2,768,2048]{2,1,0:T(8,128)(2,1)} %all-gather.8.cloned.1.call-done, f32[2,32,10,768]{3,1,2,0:T(8,128)} %fusion.4, bf16[32,2,10,2048]{3,0,2,1:T(8,128)(2,1)S(1)} %bitcast.109, bf16[2,2048,768]{2,1,0:T(8,128)(2,1)} %all-gather.6.cloned.1.call-done), kind=kOutput, calls=%fused_computation.10 | convolution fusion | flops 4030791680 | bytes 19791872 | tf_op jit(solution)/shard_map/pcrf,cfd->pcrd/dot_general | solution.py:68
  334.9 3.3 copy.43
  338.3 5.2 %fusion.13 = f32[32,12,768]{2,0,1:T(8,128)} fusion(bf16[2,2048,768]{2,1,0:T(8,128)(2,1)} %all-gather.4.cloned.1.call-done, s32[]{:T(128)S(6)} %min.4, bf16[32,12,2048]{2,1,0:T(8,128)(2,1)S(1)} %copy-done.2), kind=kOutput, calls=%fused_computation.16 | convolution fusion | flops 1207959552 | bytes 5898244 | tf_op jit(solution)/shard_map/prd,df->prf/dot_general | solution.py:60
  343.5 8.7 %fusion.18 = bf16[32,12,2048]{2,0,1:T(8,128)(2,1)} fusion(bf16[2,768,2048]{2,1,0:T(8,128)(2,1)} %all-gather.8.cloned.1.call-done, s32[]{:T(128)S(6)} %min.4, bf16[2,2048,768]{2,1,0:T(8,128)(2,1)} %all-gather.6.cloned.1.call-done, f32[32,12,768]{2,0,1:T(8,128)} %fusion.13, bf16[32,12,2048]{2,1,0:T(8,128)(2,1)} %slice.32), kind=kOutput, calls=%fused_computation.21 | convolution fusion | flops 2418475008 | bytes 11142144 | tf_op jit(solution)/shard_map/prf,fd->prd/dot_general | solution.py:69
  352.2 2.3 copy.44
  354.5 2.6 pad_maximum_fusion.1
  357.1 9.8 %all-to-all-start.1 = ((bf16[32,32,2048]{2,1,0:T(8,128)(2,1)}), bf16[32,32,2048]{2,1,0:T(8,128)(2,1)}, u32[]{:S(2)}, u32[]{:S(2)}) async-start(bf16[32,32,2048]{2,1,0:T(8,128)(2,1)} %pad_maximum_fusion.1), calls=%async_computation.1 | async-start | bytes 8388608 | tf_op jit(solution)/shard_map/all_to_all | solution.py:72
  367.6 105.7 %all-to-all-done.1 = bf16[32,32,2048]{2,1,0:T(8,128)(2,1)} async-done(((bf16[32,32,2048]{2,1,0:T(8,128)(2,1)}), bf16[32,32,2048]{2,1,0:T(8,128)(2,1)}, u32[]{:S(2)}, u32[]{:S(2)}) %all-to-all-start.1) | async-done | bytes 4194336 | tf_op jit(solution)/shard_map/all_to_all | solution.py:72
  473.3 2.1 slice.33
  475.4 2.2 reshape.161
  477.7 0.9 dynamic-slice_bitcast_fusion
  478.5 2.2 maximum_maximum_fusion
  480.8 3.3 gather_fusion
  484.1 4.5 multiply_reduce_fusion
  (37 shorter events, 1.7 us)
Async XLA Ops:
  6.5 6.3 %copy-start = (bf16[64,2048]{1,0:T(8,128)(2,1)S(1)}, bf16[64,2048]{1,0:T(8,128)(2,1)}, u32[]{:S(2)}) copy-start(bf16[64,2048]{1,0:T(8,128)(2,1)} %param.8) | copy-start | bytes 786436
  6.5 5.3 %copy-start.4 = (s32[64]{0:T(128)S(1)}, s32[64]{0:T(128)}, u32[]{:S(2)}) copy-start(s32[64]{0:T(128)} %param.11) | copy-start | bytes 772
  6.5 175.0 %all-gather.4.cloned.1.call-start = ((), (), s32[]{:S(2)}) async-start(), calls=%async_computation.2 | async-start | bytes 7077888 | tf_op jit(solution)/shard_map/all_gather | solution.py:52
  7.3 241.6 %all-gather.6.cloned.1.call-start = ((), (), s32[]{:S(2)}) async-start(), calls=%async_computation.3 | async-start | bytes 7077888 | tf_op jit(solution)/shard_map/all_gather | solution.py:53
  8.0 315.9 %all-gather.8.cloned.1.call-start = ((), (), s32[]{:S(2)}) async-start(), calls=%async_computation.4 | async-start | bytes 7077888 | tf_op jit(solution)/shard_map/all_gather | solution.py:65
  21.8 152.3 %all-to-all-start = ((bf16[32,32,2048]{2,1,0:T(8,128)(2,1)}), bf16[32,32,2048]{2,1,0:T(8,128)(2,1)}, u32[]{:S(2)}, u32[]{:S(2)}) async-start(bf16[32,32,2048]{2,1,0:T(8,128)(2,1)} %pad_maximum_fusion), calls=%async_computation | async-start | bytes 8388608 | tf_op jit(solution)/shard_map/all_to_all | solution.py:43
  334.9 3.4 copy-start.2
  357.1 10.0 %copy-start.3 = (s32[64,8]{0,1:T(8,128)S(1)}, s32[64,8]{0,1:T(8,128)}, u32[]{:S(2)}) copy-start(s32[64,8]{0,1:T(8,128)} %param.10) | copy-start | bytes 6148
  357.1 116.2 %all-to-all-start.1 = ((bf16[32,32,2048]{2,1,0:T(8,128)(2,1)}), bf16[32,32,2048]{2,1,0:T(8,128)(2,1)}, u32[]{:S(2)}, u32[]{:S(2)}) async-start(bf16[32,32,2048]{2,1,0:T(8,128)(2,1)} %pad_maximum_fusion.1), calls=%async_computation.1 | async-start | bytes 8388608 | tf_op jit(solution)/shard_map/all_to_all | solution.py:72
  480.8 7.9 %copy-start.1 = (bf16[64,2048]{1,0:T(8,128)(2,1)S(1)}, bf16[64,2048]{1,0:T(8,128)(2,1)}, u32[]{:S(2)}) copy-start(bf16[64,2048]{1,0:T(8,128)(2,1)} %param.8) | copy-start | bytes 786436
Sparse Core Ops, SparseCore 0:
  9.1 164.8 all-gather.3
  175.8 73.0 all-gather.5
  250.6 73.2 all-gather.7
where the time goes:
time: 496 us; the launch traced here: 495 us
  waiting for transfers between devices  383 us (77%)
  matrix products  33.7 us (7%)
  local copies, waits for them, and re-layouts  26.9 us (5%)
  starting transfers between devices  23 us (5%)
  other arithmetic  14.4 us (3%)
  between operations  14 us (3%)
    all_to_all x1, waiting for transfers between devices, per_device(): lax.all_to_all(jnp.concatenate([send_cap, send_hot], axis=1), 'expert', s...  139 us
    all_to_all x1, waiting for transfers between devices, per_device(): lax.all_to_all(outgoing, 'expert', split_axis=0, concat_axis=0, tiled=True)  106 us
    all_gather x1, waiting for transfers between devices, per_device(): piece = lax.all_gather(w_down, 'dp', axis=2, tiled=True)  75.1 us
    all_gather x1, waiting for transfers between devices, per_device(): piece_up = lax.all_gather(w_up, 'dp', axis=1, tiled=True)  61.1 us
    all_to_all x1, starting transfers between devices, per_device(): lax.all_to_all(jnp.concatenate([send_cap, send_hot], axis=1), 'expert', s...  13 us
    dot_general x1, matrix products, per_device(): jnp.einsum('pcrf,cfd->pcrd', hidden_cap, piece, preferred_element_type=jn...  11 us
  transfers between devices with their start and end apart: 5, of which 4 were waited for; matrix products, arithmetic and copies ran while one was open for 5% of the time, Pallas kernels for 0%

commit v1 on v0

v1 whole, which is shorter than its diff:
```python
import jax
import jax.numpy as jnp
from jax import lax
from jax.sharding import Mesh, PartitionSpec as P
from jax.experimental import pallas as pl
from jax.experimental.pallas import tpu as pltpu

SLOTS = 12
DESTS = 16
TOP = 8
VMEM_LIMIT = 56 * 1024 * 1024
BF = jnp.bfloat16
SMEM = pl.BlockSpec(memory_space=pltpu.SMEM)
VMEM = pl.BlockSpec(memory_space=pltpu.VMEM)
ANY = pl.BlockSpec(memory_space=pl.ANY)
PARAMS = pltpu.CompilerParams(vmem_limit_bytes=VMEM_LIMIT)


def pack_kernel(t_ref, r_ref, w_ref, o_ref):
    half = t_ref.shape[0] // 2
    tok = t_ref.shape[0]
    o_ref[0:half, :] = t_ref[0:half, :]
    o_ref[half + TOP :, :] = t_ref[half:, :]
    weight = w_ref[...]
    high = weight // 256
    low = weight - high * 256
    gap = jnp.zeros((TOP, 128 - tok), jnp.float32)
    parts = []
    for v in (r_ref[...], high, low):
        parts += [v.astype(jnp.float32), gap]
    used = 128 * 3
    o_ref[half : half + TOP, 0:used] = jnp.concatenate(parts, axis=1).astype(BF)
    o_ref[half : half + TOP, used:] = jnp.zeros((TOP, t_ref.shape[1] - used), BF)


def weights_kernel(s_ref, g_ref, u_ref, d_ref, mgu, ogu, md, od, bgu, bd, sem_in, sem_out):
    zp = s_ref[0]
    loads, stores = [], []
    for which in (0, 1):
        e = zp if which == 0 else 1 - zp
        gu_out, d_out = ((mgu, md), (ogu, od))[which]
        for i, src in enumerate((g_ref, u_ref)):
            loads.append(pltpu.make_async_copy(src.at[e], bgu.at[which, i], sem_in.at[which * 3 + i]))
            stores.append(
                pltpu.make_async_copy(bgu.at[which, i], gu_out.at[i], sem_out.at[which * 3 + i])
            )
        loads.append(pltpu.make_async_copy(d_ref.at[e], bd.at[which], sem_in.at[which * 3 + 2]))
        stores.append(pltpu.make_async_copy(bd.at[which], d_out, sem_out.at[which * 3 + 2]))
    for c in loads:
        c.start()
    for a, b in zip(loads, stores):
        a.wait()
        b.start()
    for b in stores:
        b.wait()


def read_meta(ref, half, tok):
    rows = ref[half : half + TOP, 0:384].astype(jnp.float32)
    return rows[:, 0:tok], rows[:, 128 : 128 + tok] * 256.0 + rows[:, 256 : 256 + tok]


def plane_experts(s_ref, cap_ref, hot_ref, tok):
    base = s_ref[1]
    row = lax.broadcasted_iota(jnp.int32, (DESTS, tok), 0)
    expert = (row // 4) * 16 + (row % 4) * 2 + base
    limit = jnp.zeros((DESTS, tok), jnp.int32)
    for d in range(DESTS):
        e = (d // 4) * 16 + (d % 4) * 2 + base
        cap = jnp.where(e == hot_ref[0], SLOTS, cap_ref[e])
        limit = jnp.where(row == d, cap, limit)
    return expert.astype(jnp.float32), limit.astype(jnp.float32)


def slots_of(named_by, expert, limit, first, tok):
    earlier = jnp.where(
        lax.broadcasted_iota(jnp.int32, (tok, tok), 0) < lax.broadcasted_iota(jnp.int32, (tok, tok), 1),
        1.0,
        0.0,
    ).astype(BF)
    named = named_by[0:1, :] == expert
    for k in range(1, TOP):
        named = jnp.logical_or(named, named_by[k : k + 1, :] == expert)
    rank = jnp.dot(jnp.where(named, 1.0, 0.0).astype(BF), earlier, preferred_element_type=jnp.float32)
    kept = jnp.logical_and(named, rank < limit)
    return jnp.where(kept, rank + first, -1.0).astype(jnp.int32)


def match_rows(slots, per, width):
    want = lax.broadcasted_iota(jnp.int32, (DESTS, per, width), 1)
    return want == slots[:, None, :]


def dispatch_kernel(s_ref, cap_ref, hot_ref, *refs):
    o_ref = refs[-1]
    refs = refs[:-1]
    far = len(refs) == 3
    half = 32
    tok = 2 * half
    per = o_ref.shape[1]
    expert, limit = plane_experts(s_ref, cap_ref, hot_ref, tok)
    slots = []
    for b, ref in enumerate(refs[:2]):
        routes, _ = read_meta(ref, half, tok)
        slots.append(slots_of(routes, expert, limit, b * SLOTS, tok))
    slots = jnp.concatenate(slots, axis=1)
    chosen = jnp.where(match_rows(slots, per, 2 * tok), 1.0, 0.0)
    chosen = chosen.reshape(DESTS * per, 2 * tok).astype(BF)
    width = o_ref.shape[2]
    step = 512
    for n in range(0, width, step):
        at = slice(n, n + step)
        rows = []
        for b, ref in enumerate(refs[:2]):
            rows.append(ref[0:half, at])
            if far and b == 1:
                rows.append(refs[2][:, at])
            else:
                rows.append(ref[half + TOP :, at])
        got = jnp.dot(chosen, jnp.concatenate(rows, axis=0), preferred_element_type=jnp.float32)
        o_ref[:, :, at] = got.astype(BF).reshape(DESTS, per, step)


def factors(s_ref, cap_ref, hot_ref, refs, per, half):
    tok = 2 * half
    expert, limit = plane_experts(s_ref, cap_ref, hot_ref, tok)
    slots, shares = [], []
    for b, ref in enumerate(refs):
        routes, weight = read_meta(ref, half, tok)
        slots.append(slots_of(routes, expert, limit, b * SLOTS, tok))
        share = weight / jnp.sum(weight, axis=0, keepdims=True)
        picked = jnp.zeros((DESTS, tok), jnp.float32)
        for k in range(TOP):
            picked = picked + jnp.where(routes[k : k + 1, :] == expert, share[k : k + 1, :], 0.0)
        shares.append(picked)
    slots = jnp.concatenate(slots, axis=1)
    shares = jnp.concatenate(shares, axis=1)
    factor = jnp.where(match_rows(slots, per, 2 * tok), shares[:, None, :], 0.0)
    factor = factor.reshape(DESTS * per, 2 * tok).T
    high = factor.astype(BF)
    low = (factor - high.astype(jnp.float32)).astype(BF)
    return high, low


def combine_kernel(s_ref, cap_ref, hot_ref, ta, tb, r_ref, *outs):
    half = 32
    per, width = r_ref.shape[1], r_ref.shape[2]
    high, low = factors(s_ref, cap_ref, hot_ref, (ta, tb), per, half)
    step = 512
    for n in range(0, width, step):
        rows = r_ref[:, :, n : n + step].reshape(DESTS * per, step)
        part = jnp.dot(high, rows, preferred_element_type=jnp.float32)
        part = part + jnp.dot(low, rows, preferred_element_type=jnp.float32)
        for i, o in enumerate(outs):
            o[:, n : n + step] = part[i * half : (i + 1) * half].astype(o.dtype)


def up_kernel(off_ref, xa_ref, xb_ref, *refs):
    groups = refs[0:8]
    ha_ref, hb_ref, wg, wu, gate_s, sems = refs[8:]
    size = groups[0].shape[1]
    copies = [[], []]
    for which, dst in enumerate((wg, wu)):
        for i in range(8):
            at = pl.multiple_of(off_ref[i] * size, size)
            copies[which].append(
                pltpu.make_async_copy(
                    groups[i].at[which], dst.at[pl.ds(at, size), :], sems.at[which * 8 + i]
                )
            )
    for group in copies:
        for c in group:
            c.start()
    rows = xa_ref.shape[0]
    step = 128
    for c in copies[0]:
        c.wait()
    for j, x_ref in enumerate((xa_ref, xb_ref)):
        for r in range(0, rows, step):
            gate_s[j * rows + r : j * rows + r + step, :] = jnp.dot(
                x_ref[r : r + step, :], wg[...], preferred_element_type=jnp.float32
            )
    for c in copies[1]:
        c.wait()
    for j, (x_ref, h_ref) in enumerate(((xa_ref, ha_ref), (xb_ref, hb_ref))):
        for r in range(0, rows, step):
            gate = gate_s[j * rows + r : j * rows + r + step, :]
            up = jnp.dot(x_ref[r : r + step, :], wu[...], preferred_element_type=jnp.float32)
            h_ref[r : r + step, :] = (gate / (1.0 + jnp.exp(-gate)) * up).astype(BF)


def down_kernel(off_ref, h_ref, *refs):
    downs = refs[0:8]
    o_ref, wd, sems = refs[8:]
    size = downs[0].shape[1]
    copies = []
    for i in range(8):
        at = pl.multiple_of(off_ref[i] * size, size)
        copies.append(pltpu.make_async_copy(downs[i], wd.at[:, pl.ds(at, size)], sems.at[i]))
    for c in copies:
        c.start()
    for c in copies:
        c.wait()
    rows = h_ref.shape[0]
    step = 128
    for r in range(0, rows, step):
        o_ref[r : r + step, :] = jnp.dot(
            h_ref[r : r + step, :], wd[...], preferred_element_type=jnp.float32
        ).astype(BF)


def cost(flops, moved, hard=0):
    return pl.CostEstimate(flops=flops, bytes_accessed=moved, transcendentals=hard)


def shape(dims, kind=BF):
    return jax.ShapeDtypeStruct(dims, kind)


def exchange(value):
    return lax.all_to_all(value, ("x", "y"), split_axis=0, concat_axis=0, tiled=True)


def per_device(tokens, routes, route_weight, capacity, hot_expert, w_gate, w_up, w_down):
    zp, zq, core, zh = (lax.axis_index(n) for n in ("zp", "zq", "core", "zh"))
    ring = ("zp", "zh")
    order = [0, 2, 1, 3]
    fwd = [(order[i], order[(i + 1) % 4]) for i in range(4)]
    back = [(order[(i + 1) % 4], order[i]) for i in range(4)]
    swap = [(0, 1), (1, 0)]
    tok, width = tokens.shape
    half = tok // 2
    ff = w_gate.shape[2]
    piece = w_gate.shape[1]
    per = 2 * SLOTS
    rows = DESTS * per
    split = half + TOP

    own = pl.pallas_call(
        pack_kernel,
        out_shape=shape((tok + TOP, width)),
        in_specs=[VMEM] * 3,
        out_specs=VMEM,
        compiler_params=PARAMS,
        cost_estimate=cost(0, 600 << 10),
        name="pack",
    )(tokens, routes.T, route_weight.T)
    tok1 = lax.ppermute(own, ring, fwd)
    tok3 = lax.ppermute(own, ring, back)

    scal = jnp.stack([zp, zh * 8 + zp]).astype(jnp.int32)
    mine_gu, other_gu, mine_d, other_d = pl.pallas_call(
        weights_kernel,
        out_shape=[shape((2, piece, ff)), shape((2, piece, ff)), shape((ff, piece)), shape((ff, piece))],
        in_specs=[SMEM, ANY, ANY, ANY],
        out_specs=[ANY] * 4,
        scratch_shapes=[
            pltpu.VMEM((2, 2, piece, ff), BF),
            pltpu.VMEM((2, ff, piece), BF),
            pltpu.SemaphoreType.DMA((6,)),
            pltpu.SemaphoreType.DMA((6,)),
        ],
        compiler_params=PARAMS,
        cost_estimate=cost(0, 5 << 20),
        name="pack_weights",
    )(scal, w_gate, w_up, w_down)

    def shards(mine, other):
        a = lax.ppermute(other, "zp", swap)
        b = lax.ppermute(mine, "zq", swap)
        c = lax.ppermute(a, "zq", swap)
        near = [lax.ppermute(v, "core", swap) for v in (mine, a, b, c)]
        return [mine, a, b, c] + near

    gates_ups = shards(mine_gu, other_gu)
    downs = shards(mine_d, other_d)

    far_top = lax.ppermute(tok1[:split], ring, fwd)
    far_low = lax.ppermute(tok3[split:], ring, back)

    def dispatch(*blocks):
        return pl.pallas_call(
            dispatch_kernel,
            out_shape=shape((DESTS, per, width)),
            in_specs=[SMEM] * 3 + [VMEM] * len(blocks),
            out_specs=VMEM,
            compiler_params=PARAMS,
            cost_estimate=cost(2 * rows * 2 * tok * width, 2 << 20),
        )(scal, capacity, hot_expert, *blocks)

    sent_b = dispatch(own, tok3)
    x_b = exchange(sent_b).reshape(rows, width)
    sent_a = dispatch(tok1, far_top, far_low)
    x_a = exchange(sent_a).reshape(rows, width)

    place = []
    for g in (0, 1):
        for b in (0, 1):
            for a in (0, 1):
                place.append((zp ^ a) * 4 + (zq ^ b) * 2 + (core ^ g))
    off = jnp.stack(place).astype(jnp.int32)
    h_a, h_b = pl.pallas_call(
        up_kernel,
        out_shape=[shape((rows, ff))] * 2,
        in_specs=[SMEM, VMEM, VMEM] + [ANY] * 8,
        out_specs=[VMEM] * 2,
        scratch_shapes=[pltpu.VMEM((width, ff), BF)] * 2
        + [pltpu.VMEM((2 * rows, ff), jnp.float32), pltpu.SemaphoreType.DMA((16,))],
        compiler_params=PARAMS,
        cost_estimate=cost(8 * rows * width * ff, 11 << 20, 2 * rows * ff),
        name="gate_up",
    )(off, x_a, x_b, *gates_ups)

    def down(h):
        out = pl.pallas_call(
            down_kernel,
            out_shape=shape((rows, width)),
            in_specs=[SMEM, VMEM] + [ANY] * 8,
            out_specs=VMEM,
            scratch_shapes=[pltpu.VMEM((ff, width), BF), pltpu.SemaphoreType.DMA((8,))],
            compiler_params=PARAMS,
            cost_estimate=cost(2 * rows * width * ff, 6 << 20),
        )(off, h, *downs)
        return out.reshape(DESTS, per, width)

    def combine(ta, tb, got, kinds):
        return pl.pallas_call(
            combine_kernel,
            out_shape=[shape((half, width), k) for k in kinds],
            in_specs=[SMEM] * 3 + [VMEM] * 3,
            out_specs=[VMEM] * len(kinds),
            compiler_params=PARAMS,
            cost_estimate=cost(4 * rows * 2 * tok * width, 3 << 20),
        )(scal, capacity, hot_expert, ta, tb, got)

    f32 = jnp.float32
    back_a = exchange(down(h_a))
    back_b = exchange(down(h_b))
    p1_top, p1_low, p2_top, p2_low = combine(tok1, far_top, back_a, (f32, BF, BF, BF))
    over_back = lax.ppermute(p2_top, ring, back)
    over_fwd = lax.ppermute(p2_low, ring, fwd)
    to_back = jnp.concatenate([(p1_top + over_back.astype(f32)).astype(BF), p1_low], axis=0)
    from_next = lax.ppermute(to_back, ring, back)
    p0_top, p0_low, p3_top, p3_low = combine(own, tok3, back_b, (f32, f32, BF, f32))
    to_fwd = jnp.concatenate([p3_top, (p3_low + over_fwd.astype(f32)).astype(BF)], axis=0)
    from_prev = lax.ppermute(to_fwd, ring, fwd)
    part0 = jnp.concatenate([p0_top, p0_low], axis=0)
    total = part0 + from_next.astype(f32) + from_prev.astype(f32)
    return total.astype(BF)


def solution(mesh):
    fine = Mesh(mesh.devices.reshape(2, 2, 2, 4, 2, 4), ("zp", "zq", "core", "x", "zh", "y"))
    dp, ex = ("zp", "zq", "core"), ("x", "zh", "y")
    in_specs = (
        P(dp + ex, None),
        P(dp + ex, None),
        P(dp + ex, None),
        P(),
        P(),
        P(ex, dp, None),
        P(ex, dp, None),
        P(ex, None, dp),
    )

    return jax.shard_map(
        per_device, mesh=fine, in_specs=in_specs, out_specs=P(dp + ex, None), check_vma=False
    )
```

time: 496 us -> 253 us (0.51)
  the two profiles are of different devices: /device:TPU:37 before, /device:TPU:32 now
where the time goes in v1:
time: 253 us
  waiting for transfers between devices  146 us (58%)
  starting transfers between devices  56.3 us (22%)
  Pallas kernels  38.9 us (15%)
  local copies, waits for them, and re-layouts  7.95 us (3%)
    ppermute x1, waiting for transfers between devices, per_device(): tok1 = lax.ppermute(own, ring, fwd)  47 us
    all_to_all x4, waiting for transfers between devices, exchange(): lax.all_to_all(value, ('x', 'y'), split_axis=0, concat_axis=0, tiled=True)  34.8 us
    all_to_all x4, starting transfers between devices, exchange(): lax.all_to_all(value, ('x', 'y'), split_axis=0, concat_axis=0, tiled=True)  24.8 us
    ppermute x2, waiting for transfers between devices, shards(): a = lax.ppermute(other, 'zp', swap)  16.8 us
    ppermute x2, waiting for transfers between devices, shards(): b = lax.ppermute(mine, 'zq', swap)  16 us
    pallas_call x2, Pallas kernels, down(): pl.pallas_call(down_kernel, out_shape=shape((rows, width)), in_specs=[SME...  11.1 us
    ppermute x1, waiting for transfers between devices, per_device(): tok3 = lax.ppermute(own, ring, back)  10.2 us
    pallas_call x1, Pallas kernels, per_device(): pl.pallas_call(up_kernel, out_shape=[shape((rows, ff))] * 2, in_specs=[SM...  9.96 us
  transfers between devices with their start and end apart: 26, of which 11 were waited for; matrix products, arithmetic and copies ran while one was open for 1% of the time, Pallas kernels for 11%

profile of v1, /device:TPU:32, one launch (start us, length us, event | category | flops | bytes accessed | tf_op | source)
XLA Modules:
  0.0 252.8 jit_solution(17934570042148491472)
XLA Ops:
  0.0 1.7 pack.1.refs_0_.ta
  1.7 5.4 %collective-permute-start = (bf16[72,2048]{1,0:T(8,128)(2,1)}, bf16[72,2048]{1,0:T(8,128)(2,1)S(1)}, u32[]{:S(2)}, u32[]{:S(2)}) collective-permute-start(bf16[72,2048]{1,0:T(8,128)(2,1)} %pack.1.refs_0_.ta), channel_id=1, source_target_pairs={{128,0},{4,128},{132,4},{0,132},{129,1},{5,129},{133,5},{1,133},{1... | collective-permute-start | bytes 884744 | tf_op jit(solution)/shard_map/ppermute | solution.py:249
  8.4 10.2 %collective-permute-done.refs_1_.tb = bf16[72,2048]{1,0:T(8,128)(2,1)S(1)} collective-permute-done((bf16[72,2048]{1,0:T(8,128)(2,1)}, bf16[72,2048]{1,0:T(8,128)(2,1)S(1)}, u32[]{:S(2)}, u32[]{:S(2)}) %collective-permute-start) | collective-permute-done | bytes 294944 | tf_op jit(solution)/shard_map/ppermute | solution.py:249
  19.3 3.0 %shard_map.83 = bf16[16,24,2048]{2,1,0:T(8,128)(2,1)} custom-call(s32[2]{0:T(128)} %pad_add_fusion.s_ref, s32[64]{0:T(128)} %cap_ref.7, s32[1]{0:T(128)S(6)} %copy.9.hot_ref, bf16[72,2048]{1,0:T(8,128)(2,1)} %pack.1.refs_0_.ta, bf16[72,2048]{1,0:T(8,128)(2,1)} %copy-done.4), custom_call_target="tpu_custom_call" | custom-call | flops 201326592 | bytes 2097152 | tf_op jit(solution)/shard_map/pallas_call | solution.py:282
  22.3 7.0 %all-to-all-start.1 = ((bf16[16,24,2048]{2,1,0:T(8,128)(2,1)}), bf16[16,24,2048]{2,1,0:T(8,128)(2,1)S(1)}, u32[]{:S(2)}, u32[]{:S(2)}) async-start(bf16[16,24,2048]{2,1,0:T(8,128)(2,1)} %shard_map.83), calls=%async_computation.1 | async-start | bytes 3145728 | tf_op jit(solution)/shard_map/all_to_all | solution.py:221
  29.3 3.3 %pack_weights.1 = (bf16[2,256,768]{2,1,0:T(8,128)(2,1)}, bf16[2,256,768]{2,1,0:T(8,128)(2,1)}, bf16[768,256]{1,0:T(8,128)(2,1)}, bf16[768,256]{1,0:T(8,128)(2,1)}) custom-call(s32[2]{0:T(128)} %pad_add_fusion.s_ref, bf16[2,256,768]{2,1,0:T(8,128)(2,1)} %g_ref.1, bf16[2,256,768]{2,1,0:T(8,128)(2,1)} %u_ref.1, bf16[2,768,256]{2,1,0:T(8,128)(2,1)} %d_ref.1), custom_call_target="tpu_custom_call" | custom-call | bytes 5242880 | tf_op jit(solution)/shard_map/pack_weights/pallas_call | solution.py:252
  33.3 2.4 collective-permute-start.1
  35.7 47.0 %collective-permute-done.1.refs_0_.ta = bf16[72,2048]{1,0:T(8,128)(2,1)S(1)} collective-permute-done((bf16[72,2048]{1,0:T(8,128)(2,1)S(1)}, bf16[72,2048]{1,0:T(8,128)(2,1)S(1)}, u32[]{:S(2)}, u32[]{:S(2)}) %collective-permute-start.1) | collective-permute-done | bytes 294944 | tf_op jit(solution)/shard_map/ppermute | solution.py:248
  82.7 3.5 %collective-permute-start.2 = (bf16[40,2048]{1,0:T(8,128)(2,1)S(1)}, bf16[40,2048]{1,0:T(8,128)(2,1)S(1)}, u32[]{:S(2)}, u32[]{:S(2)}) collective-permute-start(bf16[40,2048]{1,0:T(8,128)(2,1)S(1)} %slice.8), channel_id=1, source_target_pairs={{0,128},{128,4},{4,132},{132,0},{1,129},{129,5},{5,133},{133,1},{2... | collective-permute-start | bytes 491528 | tf_op jit(solution)/shard_map/ppermute | solution.py:278
  87.0 4.4 %collective-permute-start.3 = (bf16[32,2048]{1,0:T(8,128)(2,1)S(1)}, bf16[32,2048]{1,0:T(8,128)(2,1)S(1)}, u32[]{:S(2)}, u32[]{:S(2)}) collective-permute-start(bf16[32,2048]{1,0:T(8,128)(2,1)S(1)} %slice.9), channel_id=1, source_target_pairs={{128,0},{4,128},{132,4},{0,132},{129,1},{5,129},{133,5},{1,133},{1... | collective-permute-start | bytes 393224 | tf_op jit(solution)/shard_map/ppermute | solution.py:279
  91.4 2.0 collective-permute-start.6
  93.5 1.9 collective-permute-done.3.refs_2_
  96.6 3.0 %shard_map.82 = bf16[16,24,2048]{2,1,0:T(8,128)(2,1)} custom-call(s32[2]{0:T(128)} %pad_add_fusion.s_ref, s32[64]{0:T(128)} %cap_ref.7, s32[1]{0:T(128)S(6)} %copy.9.hot_ref, bf16[72,2048]{1,0:T(8,128)(2,1)} %copy-done.3, bf16[40,2048]{1,0:T(8,128)(2,1)} %copy-done.12, bf16[32,2048]{1,0:T(8,128)(2,1)} %copy-done.16), custom_call_target="tpu_custom_call" | custom-call | flops 201326592 | bytes 2097152 | tf_op jit(solution)/shard_map/pallas_call | solution.py:282
  99.6 7.1 %all-to-all-start = ((bf16[16,24,2048]{2,1,0:T(8,128)(2,1)}), bf16[16,24,2048]{2,1,0:T(8,128)(2,1)S(1)}, u32[]{:S(2)}, u32[]{:S(2)}) async-start(bf16[16,24,2048]{2,1,0:T(8,128)(2,1)} %shard_map.82), calls=%async_computation | async-start | bytes 3145728 | tf_op jit(solution)/shard_map/all_to_all | solution.py:221
  106.7 4.2 %collective-permute-start.11 = (bf16[768,256]{1,0:T(8,128)(2,1)}, bf16[768,256]{1,0:T(8,128)(2,1)}, u32[]{:S(2)}, u32[]{:S(2)}) collective-permute-start(bf16[768,256]{1,0:T(8,128)(2,1)} %get-tuple-element.23), channel_id=1, source_target_pairs={{0,128},{128,0},{1,129},{129,1},{2,130},{130,2},{3,131},{131,3},{4... | collective-permute-start | bytes 1179656 | tf_op jit(solution)/shard_map/ppermute | solution.py:269
  110.9 9.8 %collective-permute-done.5.refs_2_ = bf16[2,256,768]{2,1,0:T(8,128)(2,1)} collective-permute-done((bf16[2,256,768]{2,1,0:T(8,128)(2,1)}, bf16[2,256,768]{2,1,0:T(8,128)(2,1)}, u32[]{:S(2)}, u32[]{:S(2)}) %collective-permute-start.5) | collective-permute-done | bytes 786464 | tf_op jit(solution)/shard_map/ppermute | solution.py:270
  120.7 16.8 %collective-permute-done.11.refs_1_ = bf16[768,256]{1,0:T(8,128)(2,1)} collective-permute-done((bf16[768,256]{1,0:T(8,128)(2,1)}, bf16[768,256]{1,0:T(8,128)(2,1)}, u32[]{:S(2)}, u32[]{:S(2)}) %collective-permute-start.11) | collective-permute-done | bytes 393248 | tf_op jit(solution)/shard_map/ppermute | solution.py:269
  138.1 6.2 %collective-permute-done.12.refs_2_ = bf16[768,256]{1,0:T(8,128)(2,1)S(1)} collective-permute-done((bf16[768,256]{1,0:T(8,128)(2,1)S(1)}, bf16[768,256]{1,0:T(8,128)(2,1)S(1)}, u32[]{:S(2)}, u32[]{:S(2)}) %collective-permute-start.12) | collective-permute-done | bytes 393248 | tf_op jit(solution)/shard_map/ppermute | solution.py:270
  146.6 7.5 %collective-permute-done.13.refs_3_ = bf16[768,256]{1,0:T(8,128)(2,1)S(1)} collective-permute-done((bf16[768,256]{1,0:T(8,128)(2,1)}, bf16[768,256]{1,0:T(8,128)(2,1)S(1)}, u32[]{:S(2)}, u32[]{:S(2)}) %collective-permute-start.13) | collective-permute-done | bytes 393248 | tf_op jit(solution)/shard_map/ppermute | solution.py:271
  156.1 10.0 %gate_up.1 = (bf16[384,768]{1,0:T(8,128)(2,1)}, bf16[384,768]{1,0:T(8,128)(2,1)}) custom-call(s32[8]{0:T(128)} %stack.47.off_ref, bf16[384,2048]{1,0:T(8,128)(2,1)} %bitcast.19, bf16[384,2048]{1,0:T(8,128)(2,1)} %bitcast.18, bf16[2,256,768]{2,1,0:T(8,128)(2,1)} %get-tuple-element.19.refs_0_, bf16[2,256,768]{2,1,0:T(8,128)(2,1)} %collective-permute-done.4.refs_1_, ...), custom_call_target="tpu_custom_call" | custom-call | flops 4831838208 | bytes 11534336 | tf_op jit(solution)/shard_map/gate_up/pallas_call | solution.py:302
  166.9 5.5 %shard_map.86 = bf16[384,2048]{1,0:T(8,128)(2,1)} custom-call(s32[8]{0:T(128)} %stack.47.off_ref, bf16[384,768]{1,0:T(8,128)(2,1)} %get-tuple-element.26.h_ref, bf16[768,256]{1,0:T(8,128)(2,1)} %get-tuple-element.22.refs_0_, bf16[768,256]{1,0:T(8,128)(2,1)} %collective-permute-done.11.refs_1_, bf16[768,256]{1,0:T(8,128)(2,1)} %copy-done.8, ...), custom_call_target="tpu_custom_call" | custom-call | flops 1207959552 | bytes 6291456 | tf_op jit(solution)/shard_map/pallas_call | solution.py:315
  172.5 6.9 %all-to-all-start.3 = ((bf16[16,24,2048]{2,1,0:T(8,128)(2,1)}), bf16[16,24,2048]{2,1,0:T(8,128)(2,1)S(1)}, u32[]{:S(2)}, u32[]{:S(2)}) async-start(bf16[16,24,2048]{2,1,0:T(8,128)(2,1)} %bitcast.17), calls=%async_computation.3 | async-start | bytes 3145728 | tf_op jit(solution)/shard_map/all_to_all | solution.py:221
  179.4 5.6 %shard_map.84 = bf16[384,2048]{1,0:T(8,128)(2,1)} custom-call(s32[8]{0:T(128)} %stack.47.off_ref, bf16[384,768]{1,0:T(8,128)(2,1)} %get-tuple-element.21.h_ref, bf16[768,256]{1,0:T(8,128)(2,1)} %get-tuple-element.22.refs_0_, bf16[768,256]{1,0:T(8,128)(2,1)} %collective-permute-done.11.refs_1_, bf16[768,256]{1,0:T(8,128)(2,1)} %copy-done.8, ...), custom_call_target="tpu_custom_call" | custom-call | flops 1207959552 | bytes 6291456 | tf_op jit(solution)/shard_map/pallas_call | solution.py:315
  185.0 19.0 %all-to-all-done.3.r_ref = bf16[16,24,2048]{2,1,0:T(8,128)(2,1)S(1)} async-done(((bf16[16,24,2048]{2,1,0:T(8,128)(2,1)}), bf16[16,24,2048]{2,1,0:T(8,128)(2,1)S(1)}, u32[]{:S(2)}, u32[]{:S(2)}) %all-to-all-start.3) | async-done | bytes 1572896 | tf_op jit(solution)/shard_map/all_to_all | solution.py:221
  205.1 3.7 %all-to-all-start.2 = ((bf16[16,24,2048]{2,1,0:T(8,128)(2,1)}), bf16[16,24,2048]{2,1,0:T(8,128)(2,1)S(1)}, u32[]{:S(2)}, u32[]{:S(2)}) async-start(bf16[16,24,2048]{2,1,0:T(8,128)(2,1)} %bitcast.16), calls=%async_computation.2 | async-start | bytes 3145728 | tf_op jit(solution)/shard_map/all_to_all | solution.py:221
  208.8 3.4 %shard_map.87 = (f32[32,2048]{1,0:T(8,128)}, bf16[32,2048]{1,0:T(8,128)(2,1)}, bf16[32,2048]{1,0:T(8,128)(2,1)}, bf16[32,2048]{1,0:T(8,128)(2,1)}) custom-call(s32[2]{0:T(128)} %pad_add_fusion.s_ref, s32[64]{0:T(128)} %cap_ref.7, s32[1]{0:T(128)S(6)} %copy.9.hot_ref, bf16[72,2048]{1,0:T(8,128)(2,1)} %copy-done.3, bf16[40,2048]{1,0:T(8,128)(2,1)} %copy-done.12, ...), custom_call_target="tpu_custom_call" | custom-call | flops 402653184 | bytes 3145728 | tf_op jit(solution)/shard_map/pallas_call | solution.py:327
  212.2 3.0 %collective-permute-start.18 = (bf16[32,2048]{1,0:T(8,128)(2,1)}, bf16[32,2048]{1,0:T(8,128)(2,1)S(1)}, u32[]{:S(2)}, u32[]{:S(2)}) collective-permute-start(bf16[32,2048]{1,0:T(8,128)(2,1)} %get-tuple-element.28), channel_id=1, source_target_pairs={{128,0},{4,128},{132,4},{0,132},{129,1},{5,129},{133,5},{1,133},{1... | collective-permute-start | bytes 393224 | tf_op jit(solution)/shard_map/ppermute | solution.py:340
  215.2 15.9 %all-to-all-done.2.r_ref = bf16[16,24,2048]{2,1,0:T(8,128)(2,1)S(1)} async-done(((bf16[16,24,2048]{2,1,0:T(8,128)(2,1)}), bf16[16,24,2048]{2,1,0:T(8,128)(2,1)S(1)}, u32[]{:S(2)}, u32[]{:S(2)}) %all-to-all-start.2) | async-done | bytes 1572896 | tf_op jit(solution)/shard_map/all_to_all | solution.py:221
  232.2 3.5 %shard_map.85 = (f32[32,2048]{1,0:T(8,128)}, f32[32,2048]{1,0:T(8,128)}, bf16[32,2048]{1,0:T(8,128)(2,1)}, f32[32,2048]{1,0:T(8,128)}) custom-call(s32[2]{0:T(128)} %pad_add_fusion.s_ref, s32[64]{0:T(128)} %cap_ref.7, s32[1]{0:T(128)S(6)} %copy.9.hot_ref, bf16[72,2048]{1,0:T(8,128)(2,1)} %pack.1.refs_0_.ta, bf16[72,2048]{1,0:T(8,128)(2,1)} %copy-done.4, ...), custom_call_target="tpu_custom_call" | custom-call | flops 402653184 | bytes 3145728 | tf_op jit(solution)/shard_map/pallas_call | solution.py:327
  235.8 3.0 %collective-permute-start.19 = (bf16[64,2048]{1,0:T(8,128)(2,1)S(1)}, bf16[64,2048]{1,0:T(8,128)(2,1)S(1)}, u32[]{:S(2)}, u32[]{:S(2)}) collective-permute-start(bf16[64,2048]{1,0:T(8,128)(2,1)S(1)} %pad_maximum_fusion), channel_id=1, source_target_pairs={{128,0},{4,128},{132,4},{0,132},{129,1},{5,129},{133,5},{1,133},{1... | collective-permute-start | bytes 786440 | tf_op jit(solution)/shard_map/ppermute | solution.py:343
  239.9 6.6 %collective-permute-done.19 = bf16[64,2048]{1,0:T(8,128)(2,1)S(1)} collective-permute-done((bf16[64,2048]{1,0:T(8,128)(2,1)S(1)}, bf16[64,2048]{1,0:T(8,128)(2,1)S(1)}, u32[]{:S(2)}, u32[]{:S(2)}) %collective-permute-start.19) | collective-permute-done | bytes 262176 | tf_op jit(solution)/shard_map/ppermute | solution.py:343
  246.5 5.5 %collective-permute-done.21 = bf16[64,2048]{1,0:T(8,128)(2,1)S(1)} collective-permute-done((bf16[64,2048]{1,0:T(8,128)(2,1)S(1)}, bf16[64,2048]{1,0:T(8,128)(2,1)S(1)}, u32[]{:S(2)}, u32[]{:S(2)}) %collective-permute-start.21) | collective-permute-done | bytes 262176 | tf_op jit(solution)/shard_map/ppermute | solution.py:346
  (76 shorter events, 14.1 us)
Async XLA Ops:
  1.7 16.9 %collective-permute-start = (bf16[72,2048]{1,0:T(8,128)(2,1)}, bf16[72,2048]{1,0:T(8,128)(2,1)S(1)}, u32[]{:S(2)}, u32[]{:S(2)}) collective-permute-start(bf16[72,2048]{1,0:T(8,128)(2,1)} %pack.1.refs_0_.ta), channel_id=1, source_target_pairs={{128,0},{4,128},{132,4},{0,132},{129,1},{5,129},{133,5},{1,133},{1... | collective-permute-start | bytes 884744 | tf_op jit(solution)/shard_map/ppermute | solution.py:249
  22.3 77.3 %all-to-all-start.1 = ((bf16[16,24,2048]{2,1,0:T(8,128)(2,1)}), bf16[16,24,2048]{2,1,0:T(8,128)(2,1)S(1)}, u32[]{:S(2)}, u32[]{:S(2)}) async-start(bf16[16,24,2048]{2,1,0:T(8,128)(2,1)} %shard_map.83), calls=%async_computation.1 | async-start | bytes 3145728 | tf_op jit(solution)/shard_map/all_to_all | solution.py:221
  32.7 58.8 %collective-permute-start.4 = (bf16[2,256,768]{2,1,0:T(8,128)(2,1)}, bf16[2,256,768]{2,1,0:T(8,128)(2,1)}, u32[]{:S(2)}, u32[]{:S(2)}) collective-permute-start(bf16[2,256,768]{2,1,0:T(8,128)(2,1)} %get-tuple-element.20), channel_id=1, source_target_pairs={{0,128},{128,0},{1,129},{129,1},{2,130},{130,2},{3,131},{131,3},{4... | collective-permute-start | bytes 2359304 | tf_op jit(solution)/shard_map/ppermute | solution.py:269
  33.3 49.4 %collective-permute-start.1 = (bf16[72,2048]{1,0:T(8,128)(2,1)S(1)}, bf16[72,2048]{1,0:T(8,128)(2,1)S(1)}, u32[]{:S(2)}, u32[]{:S(2)}) collective-permute-start(bf16[72,2048]{1,0:T(8,128)(2,1)S(1)} %copy-done.2), channel_id=1, source_target_pairs={{0,128},{128,4},{4,132},{132,0},{1,129},{129,5},{5,133},{133,1},{2... | collective-permute-start | bytes 884744 | tf_op jit(solution)/shard_map/ppermute | solution.py:248
  82.6 12.7 %copy-start.3 = (bf16[72,2048]{1,0:T(8,128)(2,1)}, bf16[72,2048]{1,0:T(8,128)(2,1)S(1)}, u32[]{:S(2)}) copy-start(bf16[72,2048]{1,0:T(8,128)(2,1)S(1)} %collective-permute-done.1.refs_0_.ta) | copy-start | bytes 884740
  82.7 12.7 %collective-permute-start.2 = (bf16[40,2048]{1,0:T(8,128)(2,1)S(1)}, bf16[40,2048]{1,0:T(8,128)(2,1)S(1)}, u32[]{:S(2)}, u32[]{:S(2)}) collective-permute-start(bf16[40,2048]{1,0:T(8,128)(2,1)S(1)} %slice.8), channel_id=1, source_target_pairs={{0,128},{128,4},{4,132},{132,0},{1,129},{129,5},{5,133},{133,1},{2... | collective-permute-start | bytes 491528 | tf_op jit(solution)/shard_map/ppermute | solution.py:278
  87.0 8.3 %collective-permute-start.3 = (bf16[32,2048]{1,0:T(8,128)(2,1)S(1)}, bf16[32,2048]{1,0:T(8,128)(2,1)S(1)}, u32[]{:S(2)}, u32[]{:S(2)}) collective-permute-start(bf16[32,2048]{1,0:T(8,128)(2,1)S(1)} %slice.9), channel_id=1, source_target_pairs={{128,0},{4,128},{132,4},{0,132},{129,1},{5,129},{133,5},{1,133},{1... | collective-permute-start | bytes 393224 | tf_op jit(solution)/shard_map/ppermute | solution.py:279
  91.4 29.3 %collective-permute-start.5 = (bf16[2,256,768]{2,1,0:T(8,128)(2,1)}, bf16[2,256,768]{2,1,0:T(8,128)(2,1)}, u32[]{:S(2)}, u32[]{:S(2)}) collective-permute-start(bf16[2,256,768]{2,1,0:T(8,128)(2,1)} %get-tuple-element.19.refs_0_), channel_id=1, source_target_pairs={{0,64},{64,0},{1,65},{65,1},{2,66},{66,2},{3,67},{67,3},{4,68},{68... | collective-permute-start | bytes 2359304 | tf_op jit(solution)/shard_map/ppermute | solution.py:270
  91.4 46.1 %collective-permute-start.6 = (bf16[2,256,768]{2,1,0:T(8,128)(2,1)}, bf16[2,256,768]{2,1,0:T(8,128)(2,1)}, u32[]{:S(2)}, u32[]{:S(2)}) collective-permute-start(bf16[2,256,768]{2,1,0:T(8,128)(2,1)} %collective-permute-done.4.refs_1_), channel_id=1, source_target_pairs={{0,64},{64,0},{1,65},{65,1},{2,66},{66,2},{3,67},{67,3},{4,68},{68... | collective-permute-start | bytes 2359304 | tf_op jit(solution)/shard_map/ppermute | solution.py:271
  99.6 55.3 %all-to-all-start = ((bf16[16,24,2048]{2,1,0:T(8,128)(2,1)}), bf16[16,24,2048]{2,1,0:T(8,128)(2,1)S(1)}, u32[]{:S(2)}, u32[]{:S(2)}) async-start(bf16[16,24,2048]{2,1,0:T(8,128)(2,1)} %shard_map.82), calls=%async_computation | async-start | bytes 3145728 | tf_op jit(solution)/shard_map/all_to_all | solution.py:221
  106.7 30.8 %collective-permute-start.11 = (bf16[768,256]{1,0:T(8,128)(2,1)}, bf16[768,256]{1,0:T(8,128)(2,1)}, u32[]{:S(2)}, u32[]{:S(2)}) collective-permute-start(bf16[768,256]{1,0:T(8,128)(2,1)} %get-tuple-element.23), channel_id=1, source_target_pairs={{0,128},{128,0},{1,129},{129,1},{2,130},{130,2},{3,131},{131,3},{4... | collective-permute-start | bytes 1179656 | tf_op jit(solution)/shard_map/ppermute | solution.py:269
  110.9 35.7 %collective-permute-start.7 = (bf16[2,256,768]{2,1,0:T(8,128)(2,1)}, bf16[2,256,768]{2,1,0:T(8,128)(2,1)}, u32[]{:S(2)}, u32[]{:S(2)}) collective-permute-start(bf16[2,256,768]{2,1,0:T(8,128)(2,1)} %get-tuple-element.19.refs_0_), channel_id=1, source_target_pairs={{0,32},{32,0},{1,33},{33,1},{2,34},{34,2},{3,35},{35,3},{4,36},{36... | collective-permute-start | bytes 2359304 | tf_op jit(solution)/shard_map/ppermute | solution.py:272
  110.9 33.4 %collective-permute-start.12 = (bf16[768,256]{1,0:T(8,128)(2,1)S(1)}, bf16[768,256]{1,0:T(8,128)(2,1)S(1)}, u32[]{:S(2)}, u32[]{:S(2)}) collective-permute-start(bf16[768,256]{1,0:T(8,128)(2,1)S(1)} %copy-done.7), channel_id=1, source_target_pairs={{0,64},{64,0},{1,65},{65,1},{2,66},{66,2},{3,67},{67,3},{4,68},{68... | collective-permute-start | bytes 1179656 | tf_op jit(solution)/shard_map/ppermute | solution.py:270
  120.7 33.4 %collective-permute-start.9 = (bf16[2,256,768]{2,1,0:T(8,128)(2,1)}, bf16[2,256,768]{2,1,0:T(8,128)(2,1)}, u32[]{:S(2)}, u32[]{:S(2)}) collective-permute-start(bf16[2,256,768]{2,1,0:T(8,128)(2,1)} %collective-permute-done.5.refs_2_), channel_id=1, source_target_pairs={{0,32},{32,0},{1,33},{33,1},{2,34},{34,2},{3,35},{35,3},{4,36},{36... | collective-permute-start | bytes 2359304 | tf_op jit(solution)/shard_map/ppermute | solution.py:272
  137.5 17.1 %collective-permute-start.8 = (bf16[2,256,768]{2,1,0:T(8,128)(2,1)}, bf16[2,256,768]{2,1,0:T(8,128)(2,1)}, u32[]{:S(2)}, u32[]{:S(2)}) collective-permute-start(bf16[2,256,768]{2,1,0:T(8,128)(2,1)} %collective-permute-done.4.refs_1_), channel_id=1, source_target_pairs={{0,32},{32,0},{1,33},{33,1},{2,34},{34,2},{3,35},{35,3},{4,36},{36... | collective-permute-start | bytes 2359304 | tf_op jit(solution)/shard_map/ppermute | solution.py:272
  137.6 17.4 %collective-permute-start.10 = (bf16[2,256,768]{2,1,0:T(8,128)(2,1)}, bf16[2,256,768]{2,1,0:T(8,128)(2,1)}, u32[]{:S(2)}, u32[]{:S(2)}) collective-permute-start(bf16[2,256,768]{2,1,0:T(8,128)(2,1)} %collective-permute-done.6.refs_3_), channel_id=1, source_target_pairs={{0,32},{32,0},{1,33},{33,1},{2,34},{34,2},{3,35},{35,3},{4,36},{36... | collective-permute-start | bytes 2359304 | tf_op jit(solution)/shard_map/ppermute | solution.py:272
  144.3 21.8 %copy-start.8 = (bf16[768,256]{1,0:T(8,128)(2,1)}, bf16[768,256]{1,0:T(8,128)(2,1)S(1)}, u32[]{:S(2)}) copy-start(bf16[768,256]{1,0:T(8,128)(2,1)S(1)} %collective-permute-done.12.refs_2_) | copy-start | bytes 1179652
  144.3 9.8 %collective-permute-start.13 = (bf16[768,256]{1,0:T(8,128)(2,1)}, bf16[768,256]{1,0:T(8,128)(2,1)S(1)}, u32[]{:S(2)}, u32[]{:S(2)}) collective-permute-start(bf16[768,256]{1,0:T(8,128)(2,1)} %collective-permute-done.11.refs_1_), channel_id=1, source_target_pairs={{0,64},{64,0},{1,65},{65,1},{2,66},{66,2},{3,67},{67,3},{4,68},{68... | collective-permute-start | bytes 1179656 | tf_op jit(solution)/shard_map/ppermute | solution.py:271
  146.6 19.4 %collective-permute-start.14 = (bf16[768,256]{1,0:T(8,128)(2,1)S(1)}, bf16[768,256]{1,0:T(8,128)(2,1)S(1)}, u32[]{:S(2)}, u32[]{:S(2)}) collective-permute-start(bf16[768,256]{1,0:T(8,128)(2,1)S(1)} %copy-done.7), channel_id=1, source_target_pairs={{0,32},{32,0},{1,33},{33,1},{2,34},{34,2},{3,35},{35,3},{4,36},{36... | collective-permute-start | bytes 1179656 | tf_op jit(solution)/shard_map/ppermute | solution.py:272
  154.1 12.0 %collective-permute-start.15 = (bf16[768,256]{1,0:T(8,128)(2,1)}, bf16[768,256]{1,0:T(8,128)(2,1)S(1)}, u32[]{:S(2)}, u32[]{:S(2)}) collective-permute-start(bf16[768,256]{1,0:T(8,128)(2,1)} %collective-permute-done.11.refs_1_), channel_id=1, source_target_pairs={{0,32},{32,0},{1,33},{33,1},{2,34},{34,2},{3,35},{35,3},{4,36},{36... | collective-permute-start | bytes 1179656 | tf_op jit(solution)/shard_map/ppermute | solution.py:272
  154.1 11.9 %collective-permute-start.16 = (bf16[768,256]{1,0:T(8,128)(2,1)S(1)}, bf16[768,256]{1,0:T(8,128)(2,1)}, u32[]{:S(2)}, u32[]{:S(2)}) collective-permute-start(bf16[768,256]{1,0:T(8,128)(2,1)S(1)} %collective-permute-done.12.refs_2_), channel_id=1, source_target_pairs={{0,32},{32,0},{1,33},{33,1},{2,34},{34,2},{3,35},{35,3},{4,36},{36... | collective-permute-start | bytes 1179656 | tf_op jit(solution)/shard_map/ppermute | solution.py:272
  154.6 11.5 %collective-permute-start.17 = (bf16[768,256]{1,0:T(8,128)(2,1)S(1)}, bf16[768,256]{1,0:T(8,128)(2,1)}, u32[]{:S(2)}, u32[]{:S(2)}) collective-permute-start(bf16[768,256]{1,0:T(8,128)(2,1)S(1)} %collective-permute-done.13.refs_3_), channel_id=1, source_target_pairs={{0,32},{32,0},{1,33},{33,1},{2,34},{34,2},{3,35},{35,3},{4,36},{36... | collective-permute-start | bytes 1179656 | tf_op jit(solution)/shard_map/ppermute | solution.py:272
  172.5 31.5 %all-to-all-start.3 = ((bf16[16,24,2048]{2,1,0:T(8,128)(2,1)}), bf16[16,24,2048]{2,1,0:T(8,128)(2,1)S(1)}, u32[]{:S(2)}, u32[]{:S(2)}) async-start(bf16[16,24,2048]{2,1,0:T(8,128)(2,1)} %bitcast.17), calls=%async_computation.3 | async-start | bytes 3145728 | tf_op jit(solution)/shard_map/all_to_all | solution.py:221
  205.1 26.0 %all-to-all-start.2 = ((bf16[16,24,2048]{2,1,0:T(8,128)(2,1)}), bf16[16,24,2048]{2,1,0:T(8,128)(2,1)S(1)}, u32[]{:S(2)}, u32[]{:S(2)}) async-start(bf16[16,24,2048]{2,1,0:T(8,128)(2,1)} %bitcast.16), calls=%async_computation.2 | async-start | bytes 3145728 | tf_op jit(solution)/shard_map/all_to_all | solution.py:221
  212.2 23.5 %copy-start.15 = (f32[32,2048]{1,0:T(8,128)S(1)}, f32[32,2048]{1,0:T(8,128)}, u32[]{:S(2)}) copy-start(f32[32,2048]{1,0:T(8,128)} %get-tuple-element.27) | copy-start | bytes 786436
  212.2 23.6 %copy-start.17 = (bf16[32,2048]{1,0:T(8,128)(2,1)S(1)}, bf16[32,2048]{1,0:T(8,128)(2,1)}, u32[]{:S(2)}) copy-start(bf16[32,2048]{1,0:T(8,128)(2,1)} %get-tuple-element.29) | copy-start | bytes 393220
  212.2 23.5 %collective-permute-start.18 = (bf16[32,2048]{1,0:T(8,128)(2,1)}, bf16[32,2048]{1,0:T(8,128)(2,1)S(1)}, u32[]{:S(2)}, u32[]{:S(2)}) collective-permute-start(bf16[32,2048]{1,0:T(8,128)(2,1)} %get-tuple-element.28), channel_id=1, source_target_pairs={{128,0},{4,128},{132,4},{0,132},{129,1},{5,129},{133,5},{1,133},{1... | collective-permute-start | bytes 393224 | tf_op jit(solution)/shard_map/ppermute | solution.py:340
  215.2 23.6 %collective-permute-start.20 = (bf16[32,2048]{1,0:T(8,128)(2,1)}, bf16[32,2048]{1,0:T(8,128)(2,1)S(1)}, u32[]{:S(2)}, u32[]{:S(2)}) collective-permute-start(bf16[32,2048]{1,0:T(8,128)(2,1)} %get-tuple-element.32), channel_id=1, source_target_pairs={{0,128},{128,4},{4,132},{132,0},{1,129},{129,5},{5,133},{133,1},{2... | collective-permute-start | bytes 393224 | tf_op jit(solution)/shard_map/ppermute | solution.py:341
  235.7 16.3 %copy-start.13 = (f32[32,2048]{1,0:T(8,128)S(1)}, f32[32,2048]{1,0:T(8,128)}, u32[]{:S(2)}) copy-start(f32[32,2048]{1,0:T(8,128)} %get-tuple-element.24) | copy-start | bytes 786436
  235.7 16.3 %copy-start.14 = (f32[32,2048]{1,0:T(8,128)S(1)}, f32[32,2048]{1,0:T(8,128)}, u32[]{:S(2)}) copy-start(f32[32,2048]{1,0:T(8,128)} %get-tuple-element.25) | copy-start | bytes 786436
  235.8 10.7 %collective-permute-start.19 = (bf16[64,2048]{1,0:T(8,128)(2,1)S(1)}, bf16[64,2048]{1,0:T(8,128)(2,1)S(1)}, u32[]{:S(2)}, u32[]{:S(2)}) collective-permute-start(bf16[64,2048]{1,0:T(8,128)(2,1)S(1)} %pad_maximum_fusion), channel_id=1, source_target_pairs={{128,0},{4,128},{132,4},{0,132},{129,1},{5,129},{133,5},{1,133},{1... | collective-permute-start | bytes 786440 | tf_op jit(solution)/shard_map/ppermute | solution.py:343
  239.9 12.2 %collective-permute-start.21 = (bf16[64,2048]{1,0:T(8,128)(2,1)S(1)}, bf16[64,2048]{1,0:T(8,128)(2,1)S(1)}, u32[]{:S(2)}, u32[]{:S(2)}) collective-permute-start(bf16[64,2048]{1,0:T(8,128)(2,1)S(1)} %pad_maximum_fusion.1), channel_id=1, source_target_pairs={{0,128},{128,4},{4,132},{132,0},{1,129},{129,5},{5,133},{133,1},{2... | collective-permute-start | bytes 786440 | tf_op jit(solution)/shard_map/ppermute | solution.py:346
  (13 other events, 45.4 us)

commit v2 on v1

--- a/solution.py
+++ b/solution.py
@@ -8,15 +8,33 @@
 SLOTS = 12
 DESTS = 16
 TOP = 8
-VMEM_LIMIT = 56 * 1024 * 1024
 BF = jnp.bfloat16
 SMEM = pl.BlockSpec(memory_space=pltpu.SMEM)
 VMEM = pl.BlockSpec(memory_space=pltpu.VMEM)
 ANY = pl.BlockSpec(memory_space=pl.ANY)
-PARAMS = pltpu.CompilerParams(vmem_limit_bytes=VMEM_LIMIT)
-
-
-def pack_kernel(t_ref, r_ref, w_ref, o_ref):
+
+
+def grant(mib):
+    return pltpu.CompilerParams(vmem_limit_bytes=mib << 20)
+
+
+def pack_kernel(
+    s_ref, t_ref, r_ref, w_ref, g_ref, u_ref, d_ref, o_ref, mgu, ogu, md, od, bgu, bd, sem_in, sem_out
+):
+    zp = s_ref[0]
+    loads, stores = [], []
+    for which in (1, 0):
+        e = zp if which == 0 else 1 - zp
+        gu_out, d_out = ((mgu, md), (ogu, od))[which]
+        for i, src in enumerate((g_ref, u_ref)):
+            loads.append(pltpu.make_async_copy(src.at[e], bgu.at[which, i], sem_in.at[which * 3 + i]))
+            stores.append(
+                pltpu.make_async_copy(bgu.at[which, i], gu_out.at[i], sem_out.at[which * 3 + i])
+            )
+        loads.append(pltpu.make_async_copy(d_ref.at[e], bd.at[which], sem_in.at[which * 3 + 2]))
+        stores.append(pltpu.make_async_copy(bd.at[which], d_out, sem_out.at[which * 3 + 2]))
+    for c in loads:
+        c.start()
     half = t_ref.shape[0] // 2
     tok = t_ref.shape[0]
     o_ref[0:half, :] = t_ref[0:half, :]
@@ -31,23 +49,6 @@
     used = 128 * 3
     o_ref[half : half + TOP, 0:used] = jnp.concatenate(parts, axis=1).astype(BF)
     o_ref[half : half + TOP, used:] = jnp.zeros((TOP, t_ref.shape[1] - used), BF)
-
-
-def weights_kernel(s_ref, g_ref, u_ref, d_ref, mgu, ogu, md, od, bgu, bd, sem_in, sem_out):
-    zp = s_ref[0]
-    loads, stores = [], []
-    for which in (0, 1):
-        e = zp if which == 0 else 1 - zp
-        gu_out, d_out = ((mgu, md), (ogu, od))[which]
-        for i, src in enumerate((g_ref, u_ref)):
-            loads.append(pltpu.make_async_copy(src.at[e], bgu.at[which, i], sem_in.at[which * 3 + i]))
-            stores.append(
-                pltpu.make_async_copy(bgu.at[which, i], gu_out.at[i], sem_out.at[which * 3 + i])
-            )
-        loads.append(pltpu.make_async_copy(d_ref.at[e], bd.at[which], sem_in.at[which * 3 + 2]))
-        stores.append(pltpu.make_async_copy(bd.at[which], d_out, sem_out.at[which * 3 + 2]))
-    for c in loads:
-        c.start()
     for a, b in zip(loads, stores):
         a.wait()
         b.start()
@@ -92,20 +93,30 @@
 
 
 def dispatch_kernel(s_ref, cap_ref, hot_ref, *refs):
-    o_ref = refs[-1]
-    refs = refs[:-1]
+    o_ref, f_ref = refs[-2:]
+    refs = refs[:-2]
     far = len(refs) == 3
     half = 32
     tok = 2 * half
     per = o_ref.shape[1]
     expert, limit = plane_experts(s_ref, cap_ref, hot_ref, tok)
-    slots = []
+    slots, shares = [], []
     for b, ref in enumerate(refs[:2]):
-        routes, _ = read_meta(ref, half, tok)
+        routes, weight = read_meta(ref, half, tok)
         slots.append(slots_of(routes, expert, limit, b * SLOTS, tok))
+        share = weight / jnp.sum(weight, axis=0, keepdims=True)
+        picked = jnp.zeros((DESTS, tok), jnp.float32)
+        for k in range(TOP):
+            picked = picked + jnp.where(routes[k : k + 1, :] == expert, share[k : k + 1, :], 0.0)
+        shares.append(picked)
     slots = jnp.concatenate(slots, axis=1)
-    chosen = jnp.where(match_rows(slots, per, 2 * tok), 1.0, 0.0)
-    chosen = chosen.reshape(DESTS * per, 2 * tok).astype(BF)
+    shares = jnp.concatenate(shares, axis=1)
+    match = match_rows(slots, per, 2 * tok)
+    chosen = jnp.where(match, 1.0, 0.0).reshape(DESTS * per, 2 * tok).astype(BF)
+    factor = jnp.where(match, shares[:, None, :], 0.0).reshape(DESTS * per, 2 * tok).T
+    high = factor.astype(BF)
+    f_ref[0] = high
+    f_ref[1] = (factor - high.astype(jnp.float32)).astype(BF)
     width = o_ref.shape[2]
     step = 512
     for n in range(0, width, step):
@@ -121,38 +132,36 @@
         o_ref[:, :, at] = got.astype(BF).reshape(DESTS, per, step)
 
 
-def factors(s_ref, cap_ref, hot_ref, refs, per, half):
-    tok = 2 * half
-    expert, limit = plane_experts(s_ref, cap_ref, hot_ref, tok)
-    slots, shares = [], []
-    for b, ref in enumerate(refs):
-        routes, weight = read_meta(ref, half, tok)
-        slots.append(slots_of(routes, expert, limit, b * SLOTS, tok))
-        share = weight / jnp.sum(weight, axis=0, keepdims=True)
-        picked = jnp.zeros((DESTS, tok), jnp.float32)
-        for k in range(TOP):
-            picked = picked + jnp.where(routes[k : k + 1, :] == expert, share[k : k + 1, :], 0.0)
-        shares.append(picked)
-    slots = jnp.concatenate(slots, axis=1)
-    shares = jnp.concatenate(shares, axis=1)
-    factor = jnp.where(match_rows(slots, per, 2 * tok), shares[:, None, :], 0.0)
-    factor = factor.reshape(DESTS * per, 2 * tok).T
-    high = factor.astype(BF)
-    low = (factor - high.astype(jnp.float32)).astype(BF)
-    return high, low
-
-
-def combine_kernel(s_ref, cap_ref, hot_ref, ta, tb, r_ref, *outs):
+def combine_a_kernel(f_ref, r_ref, a_top, a_low, b_top, b_low):
     half = 32
     per, width = r_ref.shape[1], r_ref.shape[2]
-    high, low = factors(s_ref, cap_ref, hot_ref, (ta, tb), per, half)
     step = 512
     for n in range(0, width, step):
         rows = r_ref[:, :, n : n + step].reshape(DESTS * per, step)
-        part = jnp.dot(high, rows, preferred_element_type=jnp.float32)
-        part = part + jnp.dot(low, rows, preferred_element_type=jnp.float32)
-        for i, o in enumerate(outs):
+        part = jnp.dot(f_ref[0], rows, preferred_element_type=jnp.float32)
+        part = part + jnp.dot(f_ref[1], rows, preferred_element_type=jnp.float32)
+        for i, o in enumerate((a_top, a_low, b_top, b_low)):
             o[:, n : n + step] = part[i * half : (i + 1) * half].astype(o.dtype)
+
+
+def combine_b_kernel(f_ref, r_ref, over_ref, own_ref, out_ref):
+    half = 32
+    per, width = r_ref.shape[1], r_ref.shape[2]
+    step = 512
+    for n in range(0, width, step):
+        at = slice(n, n + step)
+        rows = r_ref[:, :, at].reshape(DESTS * per, step)
+        part = jnp.dot(f_ref[0], rows, preferred_element_type=jnp.float32)
+        part = part + jnp.dot(f_ref[1], rows, preferred_element_type=jnp.float32)
+        own_ref[:, at] = part[0 : 2 * half]
+        out_ref[0:half, at] = part[2 * half : 3 * half].astype(BF)
+        out_ref[half:, at] = (part[3 * half :] + over_ref[:, at].astype(jnp.float32)).astype(BF)
+
+
+def join_kernel(top_ref, low_ref, over_ref, out_ref):
+    half = top_ref.shape[0]
+    out_ref[0:half, :] = (top_ref[...] + over_ref[...].astype(jnp.float32)).astype(BF)
+    out_ref[half:, :] = low_ref[...]
 
 
 def up_kernel(off_ref, xa_ref, xb_ref, *refs):
@@ -193,20 +202,18 @@
     downs = refs[0:8]
     o_ref, wd, sems = refs[8:]
     size = downs[0].shape[1]
-    copies = []
-    for i in range(8):
-        at = pl.multiple_of(off_ref[i] * size, size)
-        copies.append(pltpu.make_async_copy(downs[i], wd.at[:, pl.ds(at, size)], sems.at[i]))
+    copies = [pltpu.make_async_copy(downs[i], wd.at[i], sems.at[i]) for i in range(8)]
     for c in copies:
         c.start()
-    for c in copies:
-        c.wait()
     rows = h_ref.shape[0]
     step = 128
-    for r in range(0, rows, step):
-        o_ref[r : r + step, :] = jnp.dot(
-            h_ref[r : r + step, :], wd[...], preferred_element_type=jnp.float32
-        ).astype(BF)
+    for i in range(8):
+        copies[i].wait()
+        at = pl.ds(pl.multiple_of(off_ref[i] * size, size), size)
+        for r in range(0, rows, step):
+            o_ref[r : r + step, at] = jnp.dot(
+                h_ref[r : r + step, :], wd[i], preferred_element_type=jnp.float32
+            ).astype(BF)
 
 
 def cost(flops, moved, hard=0):
@@ -236,34 +243,30 @@
     rows = DESTS * per
     split = half + TOP
 
-    own = pl.pallas_call(
+    scal = jnp.stack([zp, zh * 8 + zp]).astype(jnp.int32)
+    own, mine_gu, other_gu, mine_d, other_d = pl.pallas_call(
         pack_kernel,
-        out_shape=shape((tok + TOP, width)),
-        in_specs=[VMEM] * 3,
-        out_specs=VMEM,
-        compiler_params=PARAMS,
-        cost_estimate=cost(0, 600 << 10),
-        name="pack",
-    )(tokens, routes.T, route_weight.T)
-    tok1 = lax.ppermute(own, ring, fwd)
-    tok3 = lax.ppermute(own, ring, back)
-
-    scal = jnp.stack([zp, zh * 8 + zp]).astype(jnp.int32)
-    mine_gu, other_gu, mine_d, other_d = pl.pallas_call(
-        weights_kernel,
-        out_shape=[shape((2, piece, ff)), shape((2, piece, ff)), shape((ff, piece)), shape((ff, piece))],
-        in_specs=[SMEM, ANY, ANY, ANY],
-        out_specs=[ANY] * 4,
+        out_shape=[
+            shape((tok + TOP, width)),
+            shape((2, piece, ff)),
+            shape((2, piece, ff)),
+            shape((ff, piece)),
+            shape((ff, piece)),
+        ],
+        in_specs=[SMEM] + [VMEM] * 3 + [ANY] * 3,
+        out_specs=[VMEM] + [ANY] * 4,
         scratch_shapes=[
             pltpu.VMEM((2, 2, piece, ff), BF),
             pltpu.VMEM((2, ff, piece), BF),
             pltpu.SemaphoreType.DMA((6,)),
             pltpu.SemaphoreType.DMA((6,)),
         ],
-        compiler_params=PARAMS,
+        compiler_params=grant(56),
         cost_estimate=cost(0, 5 << 20),
-        name="pack_weights",
-    )(scal, w_gate, w_up, w_down)
+        name="pack",
+    )(scal, tokens, routes.T, route_weight.T, w_gate, w_up, w_down)
+    tok3 = lax.ppermute(own, ring, back)
+    tok1 = lax.ppermute(own, ring, fwd)
 
     def shards(mine, other):
         a = lax.ppermute(other, "zp", swap)
@@ -281,16 +284,16 @@
     def dispatch(*blocks):
         return pl.pallas_call(
             dispatch_kernel,
-            out_shape=shape((DESTS, per, width)),
+            out_shape=[shape((DESTS, per, width)), shape((2, 2 * tok, rows))],
             in_specs=[SMEM] * 3 + [VMEM] * len(blocks),
-            out_specs=VMEM,
-            compiler_params=PARAMS,
+            out_specs=[VMEM] * 2,
+            compiler_params=grant(12),
             cost_estimate=cost(2 * rows * 2 * tok * width, 2 << 20),
         )(scal, capacity, hot_expert, *blocks)
 
-    sent_b = dispatch(own, tok3)
+    sent_b, fac_b = dispatch(own, tok3)
     x_b = exchange(sent_b).reshape(rows, width)
-    sent_a = dispatch(tok1, far_top, far_low)
+    sent_a, fac_a = dispatch(tok1, far_top, far_low)
     x_a = exchange(sent_a).reshape(rows, width)
 
     place = []
@@ -306,7 +309,7 @@
         out_specs=[VMEM] * 2,
         scratch_shapes=[pltpu.VMEM((width, ff), BF)] * 2
         + [pltpu.VMEM((2 * rows, ff), jnp.float32), pltpu.SemaphoreType.DMA((16,))],
-        compiler_params=PARAMS,
+        compiler_params=grant(24),
         cost_estimate=cost(8 * rows * width * ff, 11 << 20, 2 * rows * ff),
         name="gate_up",
     )(off, x_a, x_b, *gates_ups)
@@ -317,34 +320,44 @@
             out_shape=shape((rows, width)),
             in_specs=[SMEM, VMEM] + [ANY] * 8,
             out_specs=VMEM,
-            scratch_shapes=[pltpu.VMEM((ff, width), BF), pltpu.SemaphoreType.DMA((8,))],
-            compiler_params=PARAMS,
+            scratch_shapes=[pltpu.VMEM((8, ff, piece), BF), pltpu.SemaphoreType.DMA((8,))],
+            compiler_params=grant(12),
             cost_estimate=cost(2 * rows * width * ff, 6 << 20),
         )(off, h, *downs)
         return out.reshape(DESTS, per, width)
 
-    def combine(ta, tb, got, kinds):
+    def combine(kernel, ins, outs):
         return pl.pallas_call(
-            combine_kernel,
-            out_shape=[shape((half, width), k) for k in kinds],
-            in_specs=[SMEM] * 3 + [VMEM] * 3,
-            out_specs=[VMEM] * len(kinds),
-            compiler_params=PARAMS,
+            kernel,
+            out_shape=outs,
+            in_specs=[VMEM] * len(ins),
+            out_specs=[VMEM] * len(outs),
+            compiler_params=grant(14),
             cost_estimate=cost(4 * rows * 2 * tok * width, 3 << 20),
-        )(scal, capacity, hot_expert, ta, tb, got)
+        )(*ins)
 
     f32 = jnp.float32
     back_a = exchange(down(h_a))
     back_b = exchange(down(h_b))
-    p1_top, p1_low, p2_top, p2_low = combine(tok1, far_top, back_a, (f32, BF, BF, BF))
+    p1_top, p1_low, p2_top, p2_low = combine(
+        combine_a_kernel, (fac_a, back_a), [shape((half, width), k) for k in (f32, BF, BF, BF)]
+    )
     over_back = lax.ppermute(p2_top, ring, back)
     over_fwd = lax.ppermute(p2_low, ring, fwd)
-    to_back = jnp.concatenate([(p1_top + over_back.astype(f32)).astype(BF), p1_low], axis=0)
+    to_back = pl.pallas_call(
+        join_kernel,
+        out_shape=shape((tok, width)),
+        in_specs=[VMEM] * 3,
+        out_specs=VMEM,
+        compiler_params=grant(8),
+        cost_estimate=cost(0, 700 << 10),
+        name="join",
+    )(p1_top, p1_low, over_back)
     from_next = lax.ppermute(to_back, ring, back)
-    p0_top, p0_low, p3_top, p3_low = combine(own, tok3, back_b, (f32, f32, BF, f32))
-    to_fwd = jnp.concatenate([p3_top, (p3_low + over_fwd.astype(f32)).astype(BF)], axis=0)
+    part0, to_fwd = combine(
+        combine_b_kernel, (fac_b, back_b, over_fwd), [shape((tok, width), f32), shape((tok, width))]
+    )
     from_prev = lax.ppermute(to_fwd, ring, fwd)
-    part0 = jnp.concatenate([p0_top, p0_low], axis=0)
     total = part0 + from_next.astype(f32) + from_prev.astype(f32)
     return total.astype(BF)
 

time: 253 us -> 244 us (0.964)
  the two profiles are of different devices: /device:TPU:32 before, /device:TPU:8 now
where the time goes in v2:
time: 244 us; the launch traced here: 243 us
  waiting for transfers between devices  122 us (50%)
  starting transfers between devices  81.5 us (33%)
  Pallas kernels  29.2 us (12%)
  local copies, waits for them, and re-layouts  8.26 us (3%)
    all_to_all x4, waiting for transfers between devices, exchange(): lax.all_to_all(value, ('x', 'y'), split_axis=0, concat_axis=0, tiled=True)  31 us
    ppermute x2, starting transfers between devices, shards(): b = lax.ppermute(mine, 'zq', swap)  28.1 us
    ppermute x1, waiting for transfers between devices, per_device(): tok1 = lax.ppermute(own, ring, fwd)  27.5 us
    all_to_all x4, starting transfers between devices, exchange(): lax.all_to_all(value, ('x', 'y'), split_axis=0, concat_axis=0, tiled=True)  27.2 us
    ppermute x2, waiting for transfers between devices, shards(): a = lax.ppermute(other, 'zp', swap)  25 us
    ppermute x1, waiting for transfers between devices, per_device(): tok3 = lax.ppermute(own, ring, back)  12.3 us
    pallas_call x2, Pallas kernels, down(): pl.pallas_call(down_kernel, out_shape=shape((rows, width)), in_specs=[SME...  11.2 us
    ppermute x2, waiting for transfers between devices, shards(): c = lax.ppermute(a, 'zq', swap)  11 us
  transfers between devices with their start and end apart: 26, of which 9 were waited for; matrix products, arithmetic and copies ran while one was open for 0% of the time, Pallas kernels for 7%

profile of v2, /device:TPU:8, one launch (start us, length us, event | category | flops | bytes accessed | tf_op | source)
XLA Modules:
  0.0 242.9 jit_solution(16328189758568475484)
XLA Ops:
  0.7 4.3 %pack.1 = (bf16[72,2048]{1,0:T(8,128)(2,1)}, bf16[2,256,768]{2,1,0:T(8,128)(2,1)}, bf16[2,256,768]{2,1,0:T(8,128)(2,1)}, bf16[768,256]{1,0:T(8,128)(2,1)}, bf16[768,256]{1,0:T(8,128)(2,1)}) custom-call(s32[2]{0:T(128)} %pad_add_fusion.s_ref, bf16[64,2048]{1,0:T(8,128)(2,1)} %t_ref.1, s32[8,64]{1,0:T(8,128)} %bitcast.18, s32[8,64]{1,0:T(8,128)} %bitcast.19, ...), custom_call_target="tpu_custom_call" | custom-call | bytes 5242880 | tf_op jit(solution)/shard_map/pack/pallas_call | solution.py:247
  4.9 6.4 %collective-permute-start = (bf16[72,2048]{1,0:T(8,128)(2,1)}, bf16[72,2048]{1,0:T(8,128)(2,1)S(1)}, u32[]{:S(2)}, u32[]{:S(2)}) collective-permute-start(bf16[72,2048]{1,0:T(8,128)(2,1)} %get-tuple-element.22.refs_0_), channel_id=1, source_target_pairs={{128,0},{4,128},{132,4},{0,132},{129,1},{5,129},{133,5},{1,133},{1... | collective-permute-start | bytes 884744 | tf_op jit(solution)/shard_map/ppermute | solution.py:268
  11.9 12.3 %collective-permute-done.refs_1_ = bf16[72,2048]{1,0:T(8,128)(2,1)S(1)} collective-permute-done((bf16[72,2048]{1,0:T(8,128)(2,1)}, bf16[72,2048]{1,0:T(8,128)(2,1)S(1)}, u32[]{:S(2)}, u32[]{:S(2)}) %collective-permute-start) | collective-permute-done | bytes 294944 | tf_op jit(solution)/shard_map/ppermute | solution.py:268
  24.2 1.0 copy-done.12
  25.2 2.5 %shard_map.82 = (bf16[16,24,2048]{2,1,0:T(8,128)(2,1)}, bf16[2,128,384]{2,1,0:T(8,128)(2,1)S(1)}) custom-call(s32[2]{0:T(128)S(1)} %copy-done.11, s32[64]{0:T(128)S(1)} %copy-done.14, s32[1]{0:T(128)S(6)} %copy.9.hot_ref, bf16[72,2048]{1,0:T(8,128)(2,1)S(1)} %copy-done.12, bf16[72,2048]{1,0:T(8,128)(2,1)S(1)} %collective-permute-done.refs_1_), custom_call_target="tpu_custom_call" | custom-call | flops 201326592 | bytes 2097152 | tf_op jit(solution)/shard_map/pallas_call | solution.py:285
  28.3 7.5 %all-to-all-start.1 = ((bf16[16,24,2048]{2,1,0:T(8,128)(2,1)}), bf16[16,24,2048]{2,1,0:T(8,128)(2,1)S(1)}, u32[]{:S(2)}, u32[]{:S(2)}) async-start(bf16[16,24,2048]{2,1,0:T(8,128)(2,1)} %get-tuple-element.25), calls=%async_computation.1 | async-start | bytes 3145728 | tf_op jit(solution)/shard_map/all_to_all | solution.py:228
  35.9 2.1 collective-permute-start.4
  38.9 27.5 %collective-permute-done.1.refs_0_ = bf16[72,2048]{1,0:T(8,128)(2,1)S(1)} collective-permute-done((bf16[72,2048]{1,0:T(8,128)(2,1)S(1)}, bf16[72,2048]{1,0:T(8,128)(2,1)S(1)}, u32[]{:S(2)}, u32[]{:S(2)}) %collective-permute-start.1) | collective-permute-done | bytes 294944 | tf_op jit(solution)/shard_map/ppermute | solution.py:269
  66.4 3.5 %collective-permute-start.2 = (bf16[40,2048]{1,0:T(8,128)(2,1)S(1)}, bf16[40,2048]{1,0:T(8,128)(2,1)S(1)}, u32[]{:S(2)}, u32[]{:S(2)}) collective-permute-start(bf16[40,2048]{1,0:T(8,128)(2,1)S(1)} %slice.8), channel_id=1, source_target_pairs={{0,128},{128,4},{4,132},{132,0},{1,129},{129,5},{5,133},{133,1},{2... | collective-permute-start | bytes 491528 | tf_op jit(solution)/shard_map/ppermute | solution.py:281
  69.9 2.6 %collective-permute-start.3 = (bf16[32,2048]{1,0:T(8,128)(2,1)S(1)}, bf16[32,2048]{1,0:T(8,128)(2,1)S(1)}, u32[]{:S(2)}, u32[]{:S(2)}) collective-permute-start(bf16[32,2048]{1,0:T(8,128)(2,1)S(1)} %slice.9), channel_id=1, source_target_pairs={{128,0},{4,128},{132,4},{0,132},{129,1},{5,129},{133,5},{1,133},{1... | collective-permute-start | bytes 393224 | tf_op jit(solution)/shard_map/ppermute | solution.py:282
  72.5 20.3 %collective-permute-start.5 = (bf16[2,256,768]{2,1,0:T(8,128)(2,1)}, bf16[2,256,768]{2,1,0:T(8,128)(2,1)}, u32[]{:S(2)}, u32[]{:S(2)}) collective-permute-start(bf16[2,256,768]{2,1,0:T(8,128)(2,1)} %get-tuple-element.26.refs_0_), channel_id=1, source_target_pairs={{0,64},{64,0},{1,65},{65,1},{2,66},{66,2},{3,67},{67,3},{4,68},{68... | collective-permute-start | bytes 2359304 | tf_op jit(solution)/shard_map/ppermute | solution.py:273
  92.8 1.3 shard_map.83
  94.2 1.2 copy-done
  96.0 7.4 %all-to-all-start = ((bf16[16,24,2048]{2,1,0:T(8,128)(2,1)}), bf16[16,24,2048]{2,1,0:T(8,128)(2,1)S(1)}, u32[]{:S(2)}, u32[]{:S(2)}) async-start(bf16[16,24,2048]{2,1,0:T(8,128)(2,1)} %copy-done), calls=%async_computation | async-start | bytes 3145728 | tf_op jit(solution)/shard_map/all_to_all | solution.py:228
  103.5 7.9 %collective-permute-start.12 = (bf16[768,256]{1,0:T(8,128)(2,1)S(1)}, bf16[768,256]{1,0:T(8,128)(2,1)S(1)}, u32[]{:S(2)}, u32[]{:S(2)}) collective-permute-start(bf16[768,256]{1,0:T(8,128)(2,1)S(1)} %copy-done.1), channel_id=1, source_target_pairs={{0,64},{64,0},{1,65},{65,1},{2,66},{66,2},{3,67},{67,3},{4,68},{68... | collective-permute-start | bytes 1179656 | tf_op jit(solution)/shard_map/ppermute | solution.py:273
  111.3 25.0 %collective-permute-done.11.refs_1_ = bf16[768,256]{1,0:T(8,128)(2,1)} collective-permute-done((bf16[768,256]{1,0:T(8,128)(2,1)}, bf16[768,256]{1,0:T(8,128)(2,1)}, u32[]{:S(2)}, u32[]{:S(2)}) %collective-permute-start.11) | collective-permute-done | bytes 393248 | tf_op jit(solution)/shard_map/ppermute | solution.py:272
  136.8 2.5 %collective-permute-done.6.refs_3_ = bf16[2,256,768]{2,1,0:T(8,128)(2,1)} collective-permute-done((bf16[2,256,768]{2,1,0:T(8,128)(2,1)}, bf16[2,256,768]{2,1,0:T(8,128)(2,1)}, u32[]{:S(2)}, u32[]{:S(2)}) %collective-permute-start.6) | collective-permute-done | bytes 786464 | tf_op jit(solution)/shard_map/ppermute | solution.py:274
  139.4 5.8 %collective-permute-done.12.refs_2_ = bf16[768,256]{1,0:T(8,128)(2,1)S(1)} collective-permute-done((bf16[768,256]{1,0:T(8,128)(2,1)S(1)}, bf16[768,256]{1,0:T(8,128)(2,1)S(1)}, u32[]{:S(2)}, u32[]{:S(2)}) %collective-permute-start.12) | collective-permute-done | bytes 393248 | tf_op jit(solution)/shard_map/ppermute | solution.py:273
  147.0 8.5 %collective-permute-done.13.refs_3_ = bf16[768,256]{1,0:T(8,128)(2,1)} collective-permute-done((bf16[768,256]{1,0:T(8,128)(2,1)}, bf16[768,256]{1,0:T(8,128)(2,1)}, u32[]{:S(2)}, u32[]{:S(2)}) %collective-permute-start.13) | collective-permute-done | bytes 393248 | tf_op jit(solution)/shard_map/ppermute | solution.py:274
  156.1 7.8 %gate_up.1 = (bf16[384,768]{1,0:T(8,128)(2,1)S(1)}, bf16[384,768]{1,0:T(8,128)(2,1)S(1)}) custom-call(s32[8]{0:T(128)S(1)} %stack.47.off_ref, bf16[384,2048]{1,0:T(8,128)(2,1)S(1)} %bitcast.17, bf16[384,2048]{1,0:T(8,128)(2,1)S(1)} %bitcast.16, bf16[2,256,768]{2,1,0:T(8,128)(2,1)} %get-tuple-element.26.refs_0_, ...), custom_call_target="tpu_custom_call" | custom-call | flops 4831838208 | bytes 11534336 | tf_op jit(solution)/shard_map/gate_up/pallas_call | solution.py:305
  164.0 5.6 %shard_map.85 = bf16[384,2048]{1,0:T(8,128)(2,1)} custom-call(s32[8]{0:T(128)S(1)} %stack.47.off_ref, bf16[384,768]{1,0:T(8,128)(2,1)S(1)} %get-tuple-element.32.h_ref, bf16[768,256]{1,0:T(8,128)(2,1)S(1)} %copy-done.1, bf16[768,256]{1,0:T(8,128)(2,1)} %collective-permute-done.11.refs_1_, bf16[768,256]{1,0:T(8,128)(2,1)S(1)} %copy-done.3, ...), custom_call_target="tpu_custom_call" | custom-call | flops 1207959552 | bytes 6291456 | tf_op jit(solution)/shard_map/pallas_call | solution.py:318
  169.6 7.2 %all-to-all-start.3 = ((bf16[16,24,2048]{2,1,0:T(8,128)(2,1)}), bf16[16,24,2048]{2,1,0:T(8,128)(2,1)S(1)}, u32[]{:S(2)}, u32[]{:S(2)}) async-start(bf16[16,24,2048]{2,1,0:T(8,128)(2,1)} %bitcast.15), calls=%async_computation.3 | async-start | bytes 3145728 | tf_op jit(solution)/shard_map/all_to_all | solution.py:228
  176.8 1.0 copy-done.4
  177.8 1.1 copy-done.6
  178.9 5.6 %shard_map.84 = bf16[384,2048]{1,0:T(8,128)(2,1)} custom-call(s32[8]{0:T(128)S(1)} %stack.47.off_ref, bf16[384,768]{1,0:T(8,128)(2,1)S(1)} %copy-done.6, bf16[768,256]{1,0:T(8,128)(2,1)S(1)} %copy-done.1, bf16[768,256]{1,0:T(8,128)(2,1)} %collective-permute-done.11.refs_1_, bf16[768,256]{1,0:T(8,128)(2,1)S(1)} %copy-done.4, ...), custom_call_target="tpu_custom_call" | custom-call | flops 1207959552 | bytes 6291456 | tf_op jit(solution)/shard_map/pallas_call | solution.py:318
  184.5 15.8 %all-to-all-done.3.r_ref = bf16[16,24,2048]{2,1,0:T(8,128)(2,1)S(1)} async-done(((bf16[16,24,2048]{2,1,0:T(8,128)(2,1)}), bf16[16,24,2048]{2,1,0:T(8,128)(2,1)S(1)}, u32[]{:S(2)}, u32[]{:S(2)}) %all-to-all-start.3) | async-done | bytes 1572896 | tf_op jit(solution)/shard_map/all_to_all | solution.py:228
  200.3 5.1 %all-to-all-start.2 = ((bf16[16,24,2048]{2,1,0:T(8,128)(2,1)}), bf16[16,24,2048]{2,1,0:T(8,128)(2,1)S(1)}, u32[]{:S(2)}, u32[]{:S(2)}) async-start(bf16[16,24,2048]{2,1,0:T(8,128)(2,1)} %bitcast.14), calls=%async_computation.2 | async-start | bytes 3145728 | tf_op jit(solution)/shard_map/all_to_all | solution.py:228
  206.4 1.4 shard_map.86
  207.8 4.1 %collective-permute-start.19 = (bf16[32,2048]{1,0:T(8,128)(2,1)}, bf16[32,2048]{1,0:T(8,128)(2,1)S(1)}, u32[]{:S(2)}, u32[]{:S(2)}) collective-permute-start(bf16[32,2048]{1,0:T(8,128)(2,1)} %get-tuple-element.37), channel_id=1, source_target_pairs={{128,0},{4,128},{132,4},{0,132},{129,1},{5,129},{133,5},{1,133},{1... | collective-permute-start | bytes 393224 | tf_op jit(solution)/shard_map/ppermute | solution.py:345
  211.9 15.2 %all-to-all-done.2.r_ref = bf16[16,24,2048]{2,1,0:T(8,128)(2,1)S(1)} async-done(((bf16[16,24,2048]{2,1,0:T(8,128)(2,1)}), bf16[16,24,2048]{2,1,0:T(8,128)(2,1)S(1)}, u32[]{:S(2)}, u32[]{:S(2)}) %all-to-all-start.2) | async-done | bytes 1572896 | tf_op jit(solution)/shard_map/all_to_all | solution.py:228
  228.9 4.2 %collective-permute-start.20 = (bf16[64,2048]{1,0:T(8,128)(2,1)S(1)}, bf16[64,2048]{1,0:T(8,128)(2,1)S(1)}, u32[]{:S(2)}, u32[]{:S(2)}) collective-permute-start(bf16[64,2048]{1,0:T(8,128)(2,1)S(1)} %join.1), channel_id=1, source_target_pairs={{128,0},{4,128},{132,4},{0,132},{129,1},{5,129},{133,5},{1,133},{1... | collective-permute-start | bytes 786440 | tf_op jit(solution)/shard_map/ppermute | solution.py:356
  233.1 9.0 %collective-permute-done.21 = bf16[64,2048]{1,0:T(8,128)(2,1)S(1)} collective-permute-done((bf16[64,2048]{1,0:T(8,128)(2,1)S(1)}, bf16[64,2048]{1,0:T(8,128)(2,1)S(1)}, u32[]{:S(2)}, u32[]{:S(2)}) %collective-permute-start.21) | collective-permute-done | bytes 262176 | tf_op jit(solution)/shard_map/ppermute | solution.py:360
  (66 shorter events, 9.5 us)
Async XLA Ops:
  0.0 24.2 %copy-start.14 = (s32[64]{0:T(128)S(1)}, s32[64]{0:T(128)}, u32[]{:S(2)}) copy-start(s32[64]{0:T(128)} %cap_ref.3) | copy-start | bytes 772
  0.7 23.6 %copy-start.11 = (s32[2]{0:T(128)S(1)}, s32[2]{0:T(128)}, u32[]{:S(2)}) copy-start(s32[2]{0:T(128)} %pad_add_fusion.s_ref) | copy-start | bytes 28
  4.9 19.3 %collective-permute-start = (bf16[72,2048]{1,0:T(8,128)(2,1)}, bf16[72,2048]{1,0:T(8,128)(2,1)S(1)}, u32[]{:S(2)}, u32[]{:S(2)}) collective-permute-start(bf16[72,2048]{1,0:T(8,128)(2,1)} %get-tuple-element.22.refs_0_), channel_id=1, source_target_pairs={{128,0},{4,128},{132,4},{0,132},{129,1},{5,129},{133,5},{1,133},{1... | collective-permute-start | bytes 884744 | tf_op jit(solution)/shard_map/ppermute | solution.py:268
  28.3 7.5 %copy-start.15 = (bf16[2,256,768]{2,1,0:T(8,128)(2,1)S(1)}, bf16[2,256,768]{2,1,0:T(8,128)(2,1)}, u32[]{:S(2)}) copy-start(bf16[2,256,768]{2,1,0:T(8,128)(2,1)} %get-tuple-element.27) | copy-start | bytes 2359300
  28.3 9.7 %copy-start.13 = (bf16[72,2048]{1,0:T(8,128)(2,1)S(1)}, bf16[72,2048]{1,0:T(8,128)(2,1)}, u32[]{:S(2)}) copy-start(bf16[72,2048]{1,0:T(8,128)(2,1)} %get-tuple-element.22.refs_0_) | copy-start | bytes 884740
  28.3 67.7 %all-to-all-start.1 = ((bf16[16,24,2048]{2,1,0:T(8,128)(2,1)}), bf16[16,24,2048]{2,1,0:T(8,128)(2,1)S(1)}, u32[]{:S(2)}, u32[]{:S(2)}) async-start(bf16[16,24,2048]{2,1,0:T(8,128)(2,1)} %get-tuple-element.25), calls=%async_computation.1 | async-start | bytes 3145728 | tf_op jit(solution)/shard_map/all_to_all | solution.py:228
  35.9 56.9 %collective-permute-start.4 = (bf16[2,256,768]{2,1,0:T(8,128)(2,1)S(1)}, bf16[2,256,768]{2,1,0:T(8,128)(2,1)}, u32[]{:S(2)}, u32[]{:S(2)}) collective-permute-start(bf16[2,256,768]{2,1,0:T(8,128)(2,1)S(1)} %copy-done.15), channel_id=1, source_target_pairs={{0,128},{128,0},{1,129},{129,1},{2,130},{130,2},{3,131},{131,3},{4... | collective-permute-start | bytes 2359304 | tf_op jit(solution)/shard_map/ppermute | solution.py:272
  38.0 28.4 %collective-permute-start.1 = (bf16[72,2048]{1,0:T(8,128)(2,1)S(1)}, bf16[72,2048]{1,0:T(8,128)(2,1)S(1)}, u32[]{:S(2)}, u32[]{:S(2)}) collective-permute-start(bf16[72,2048]{1,0:T(8,128)(2,1)S(1)} %copy-done.13), channel_id=1, source_target_pairs={{0,128},{128,4},{4,132},{132,0},{1,129},{129,5},{5,133},{133,1},{2... | collective-permute-start | bytes 884744 | tf_op jit(solution)/shard_map/ppermute | solution.py:269
  66.4 26.4 %collective-permute-start.2 = (bf16[40,2048]{1,0:T(8,128)(2,1)S(1)}, bf16[40,2048]{1,0:T(8,128)(2,1)S(1)}, u32[]{:S(2)}, u32[]{:S(2)}) collective-permute-start(bf16[40,2048]{1,0:T(8,128)(2,1)S(1)} %slice.8), channel_id=1, source_target_pairs={{0,128},{128,4},{4,132},{132,0},{1,129},{129,5},{5,133},{133,1},{2... | collective-permute-start | bytes 491528 | tf_op jit(solution)/shard_map/ppermute | solution.py:281
  69.9 22.9 %collective-permute-start.3 = (bf16[32,2048]{1,0:T(8,128)(2,1)S(1)}, bf16[32,2048]{1,0:T(8,128)(2,1)S(1)}, u32[]{:S(2)}, u32[]{:S(2)}) collective-permute-start(bf16[32,2048]{1,0:T(8,128)(2,1)S(1)} %slice.9), channel_id=1, source_target_pairs={{128,0},{4,128},{132,4},{0,132},{129,1},{5,129},{133,5},{1,133},{1... | collective-permute-start | bytes 393224 | tf_op jit(solution)/shard_map/ppermute | solution.py:282
  72.5 63.8 %collective-permute-start.5 = (bf16[2,256,768]{2,1,0:T(8,128)(2,1)}, bf16[2,256,768]{2,1,0:T(8,128)(2,1)}, u32[]{:S(2)}, u32[]{:S(2)}) collective-permute-start(bf16[2,256,768]{2,1,0:T(8,128)(2,1)} %get-tuple-element.26.refs_0_), channel_id=1, source_target_pairs={{0,64},{64,0},{1,65},{65,1},{2,66},{66,2},{3,67},{67,3},{4,68},{68... | collective-permute-start | bytes 2359304 | tf_op jit(solution)/shard_map/ppermute | solution.py:273
  92.8 46.6 %collective-permute-start.6 = (bf16[2,256,768]{2,1,0:T(8,128)(2,1)}, bf16[2,256,768]{2,1,0:T(8,128)(2,1)}, u32[]{:S(2)}, u32[]{:S(2)}) collective-permute-start(bf16[2,256,768]{2,1,0:T(8,128)(2,1)} %collective-permute-done.4.refs_1_), channel_id=1, source_target_pairs={{0,64},{64,0},{1,65},{65,1},{2,66},{66,2},{3,67},{67,3},{4,68},{68... | collective-permute-start | bytes 2359304 | tf_op jit(solution)/shard_map/ppermute | solution.py:274
  96.0 7.5 %copy-start.1 = (bf16[768,256]{1,0:T(8,128)(2,1)S(1)}, bf16[768,256]{1,0:T(8,128)(2,1)}, u32[]{:S(2)}) copy-start(bf16[768,256]{1,0:T(8,128)(2,1)} %get-tuple-element.29.refs_0_) | copy-start | bytes 1179652
  96.0 60.1 %all-to-all-start = ((bf16[16,24,2048]{2,1,0:T(8,128)(2,1)}), bf16[16,24,2048]{2,1,0:T(8,128)(2,1)S(1)}, u32[]{:S(2)}, u32[]{:S(2)}) async-start(bf16[16,24,2048]{2,1,0:T(8,128)(2,1)} %copy-done), calls=%async_computation | async-start | bytes 3145728 | tf_op jit(solution)/shard_map/all_to_all | solution.py:228
  103.4 33.0 %collective-permute-start.11 = (bf16[768,256]{1,0:T(8,128)(2,1)}, bf16[768,256]{1,0:T(8,128)(2,1)}, u32[]{:S(2)}, u32[]{:S(2)}) collective-permute-start(bf16[768,256]{1,0:T(8,128)(2,1)} %get-tuple-element.30), channel_id=1, source_target_pairs={{0,128},{128,0},{1,129},{129,1},{2,130},{130,2},{3,131},{131,3},{4... | collective-permute-start | bytes 1179656 | tf_op jit(solution)/shard_map/ppermute | solution.py:272
  103.4 43.6 %collective-permute-start.7 = (bf16[2,256,768]{2,1,0:T(8,128)(2,1)}, bf16[2,256,768]{2,1,0:T(8,128)(2,1)}, u32[]{:S(2)}, u32[]{:S(2)}) collective-permute-start(bf16[2,256,768]{2,1,0:T(8,128)(2,1)} %get-tuple-element.26.refs_0_), channel_id=1, source_target_pairs={{0,32},{32,0},{1,33},{33,1},{2,34},{34,2},{3,35},{35,3},{4,36},{36... | collective-permute-start | bytes 2359304 | tf_op jit(solution)/shard_map/ppermute | solution.py:275
  103.5 41.7 %collective-permute-start.12 = (bf16[768,256]{1,0:T(8,128)(2,1)S(1)}, bf16[768,256]{1,0:T(8,128)(2,1)S(1)}, u32[]{:S(2)}, u32[]{:S(2)}) collective-permute-start(bf16[768,256]{1,0:T(8,128)(2,1)S(1)} %copy-done.1), channel_id=1, source_target_pairs={{0,64},{64,0},{1,65},{65,1},{2,66},{66,2},{3,67},{67,3},{4,68},{68... | collective-permute-start | bytes 1179656 | tf_op jit(solution)/shard_map/ppermute | solution.py:273
  136.3 19.2 %collective-permute-start.8 = (bf16[2,256,768]{2,1,0:T(8,128)(2,1)}, bf16[2,256,768]{2,1,0:T(8,128)(2,1)}, u32[]{:S(2)}, u32[]{:S(2)}) collective-permute-start(bf16[2,256,768]{2,1,0:T(8,128)(2,1)} %collective-permute-done.4.refs_1_), channel_id=1, source_target_pairs={{0,32},{32,0},{1,33},{33,1},{2,34},{34,2},{3,35},{35,3},{4,36},{36... | collective-permute-start | bytes 2359304 | tf_op jit(solution)/shard_map/ppermute | solution.py:275
  136.3 19.7 %collective-permute-start.9 = (bf16[2,256,768]{2,1,0:T(8,128)(2,1)}, bf16[2,256,768]{2,1,0:T(8,128)(2,1)}, u32[]{:S(2)}, u32[]{:S(2)}) collective-permute-start(bf16[2,256,768]{2,1,0:T(8,128)(2,1)} %collective-permute-done.5.refs_2_), channel_id=1, source_target_pairs={{0,32},{32,0},{1,33},{33,1},{2,34},{34,2},{3,35},{35,3},{4,36},{36... | collective-permute-start | bytes 2359304 | tf_op jit(solution)/shard_map/ppermute | solution.py:275
  139.4 16.7 %collective-permute-start.10 = (bf16[2,256,768]{2,1,0:T(8,128)(2,1)}, bf16[2,256,768]{2,1,0:T(8,128)(2,1)}, u32[]{:S(2)}, u32[]{:S(2)}) collective-permute-start(bf16[2,256,768]{2,1,0:T(8,128)(2,1)} %collective-permute-done.6.refs_3_), channel_id=1, source_target_pairs={{0,32},{32,0},{1,33},{33,1},{2,34},{34,2},{3,35},{35,3},{4,36},{36... | collective-permute-start | bytes 2359304 | tf_op jit(solution)/shard_map/ppermute | solution.py:275
  145.9 9.6 %collective-permute-start.13 = (bf16[768,256]{1,0:T(8,128)(2,1)}, bf16[768,256]{1,0:T(8,128)(2,1)}, u32[]{:S(2)}, u32[]{:S(2)}) collective-permute-start(bf16[768,256]{1,0:T(8,128)(2,1)} %collective-permute-done.11.refs_1_), channel_id=1, source_target_pairs={{0,64},{64,0},{1,65},{65,1},{2,66},{66,2},{3,67},{67,3},{4,68},{68... | collective-permute-start | bytes 1179656 | tf_op jit(solution)/shard_map/ppermute | solution.py:274
  146.9 17.0 %collective-permute-start.14 = (bf16[768,256]{1,0:T(8,128)(2,1)S(1)}, bf16[768,256]{1,0:T(8,128)(2,1)}, u32[]{:S(2)}, u32[]{:S(2)}) collective-permute-start(bf16[768,256]{1,0:T(8,128)(2,1)S(1)} %copy-done.1), channel_id=1, source_target_pairs={{0,32},{32,0},{1,33},{33,1},{2,34},{34,2},{3,35},{35,3},{4,36},{36... | collective-permute-start | bytes 1179656 | tf_op jit(solution)/shard_map/ppermute | solution.py:275
  155.5 8.4 %collective-permute-start.15 = (bf16[768,256]{1,0:T(8,128)(2,1)}, bf16[768,256]{1,0:T(8,128)(2,1)}, u32[]{:S(2)}, u32[]{:S(2)}) collective-permute-start(bf16[768,256]{1,0:T(8,128)(2,1)} %collective-permute-done.11.refs_1_), channel_id=1, source_target_pairs={{0,32},{32,0},{1,33},{33,1},{2,34},{34,2},{3,35},{35,3},{4,36},{36... | collective-permute-start | bytes 1179656 | tf_op jit(solution)/shard_map/ppermute | solution.py:275
  155.5 8.4 %collective-permute-start.16 = (bf16[768,256]{1,0:T(8,128)(2,1)}, bf16[768,256]{1,0:T(8,128)(2,1)}, u32[]{:S(2)}, u32[]{:S(2)}) collective-permute-start(bf16[768,256]{1,0:T(8,128)(2,1)} %copy-done.2), channel_id=1, source_target_pairs={{0,32},{32,0},{1,33},{33,1},{2,34},{34,2},{3,35},{35,3},{4,36},{36... | collective-permute-start | bytes 1179656 | tf_op jit(solution)/shard_map/ppermute | solution.py:275
  156.0 7.9 %collective-permute-start.17 = (bf16[768,256]{1,0:T(8,128)(2,1)}, bf16[768,256]{1,0:T(8,128)(2,1)}, u32[]{:S(2)}, u32[]{:S(2)}) collective-permute-start(bf16[768,256]{1,0:T(8,128)(2,1)} %collective-permute-done.13.refs_3_), channel_id=1, source_target_pairs={{0,32},{32,0},{1,33},{33,1},{2,34},{34,2},{3,35},{35,3},{4,36},{36... | collective-permute-start | bytes 1179656 | tf_op jit(solution)/shard_map/ppermute | solution.py:275
  156.1 7.8 %copy-start.3 = (bf16[768,256]{1,0:T(8,128)(2,1)S(1)}, bf16[768,256]{1,0:T(8,128)(2,1)}, u32[]{:S(2)}) copy-start(bf16[768,256]{1,0:T(8,128)(2,1)} %copy-done.2) | copy-start | bytes 1179652
  169.6 30.7 %all-to-all-start.3 = ((bf16[16,24,2048]{2,1,0:T(8,128)(2,1)}), bf16[16,24,2048]{2,1,0:T(8,128)(2,1)S(1)}, u32[]{:S(2)}, u32[]{:S(2)}) async-start(bf16[16,24,2048]{2,1,0:T(8,128)(2,1)} %bitcast.15), calls=%async_computation.3 | async-start | bytes 3145728 | tf_op jit(solution)/shard_map/all_to_all | solution.py:228
  200.3 26.7 %all-to-all-start.2 = ((bf16[16,24,2048]{2,1,0:T(8,128)(2,1)}), bf16[16,24,2048]{2,1,0:T(8,128)(2,1)S(1)}, u32[]{:S(2)}, u32[]{:S(2)}) async-start(bf16[16,24,2048]{2,1,0:T(8,128)(2,1)} %bitcast.14), calls=%async_computation.2 | async-start | bytes 3145728 | tf_op jit(solution)/shard_map/all_to_all | solution.py:228
  207.8 19.3 %collective-permute-start.18 = (bf16[32,2048]{1,0:T(8,128)(2,1)}, bf16[32,2048]{1,0:T(8,128)(2,1)S(1)}, u32[]{:S(2)}, u32[]{:S(2)}) collective-permute-start(bf16[32,2048]{1,0:T(8,128)(2,1)} %get-tuple-element.33), channel_id=1, source_target_pairs={{0,128},{128,4},{4,132},{132,0},{1,129},{129,5},{5,133},{133,1},{2... | collective-permute-start | bytes 393224 | tf_op jit(solution)/shard_map/ppermute | solution.py:346
  207.8 21.0 %collective-permute-start.19 = (bf16[32,2048]{1,0:T(8,128)(2,1)}, bf16[32,2048]{1,0:T(8,128)(2,1)S(1)}, u32[]{:S(2)}, u32[]{:S(2)}) collective-permute-start(bf16[32,2048]{1,0:T(8,128)(2,1)} %get-tuple-element.37), channel_id=1, source_target_pairs={{128,0},{4,128},{132,4},{0,132},{129,1},{5,129},{133,5},{1,133},{1... | collective-permute-start | bytes 393224 | tf_op jit(solution)/shard_map/ppermute | solution.py:345
  228.7 13.4 %collective-permute-start.21 = (bf16[64,2048]{1,0:T(8,128)(2,1)S(1)}, bf16[64,2048]{1,0:T(8,128)(2,1)S(1)}, u32[]{:S(2)}, u32[]{:S(2)}) collective-permute-start(bf16[64,2048]{1,0:T(8,128)(2,1)S(1)} %get-tuple-element.38), channel_id=1, source_target_pairs={{0,128},{128,4},{4,132},{132,0},{1,129},{129,5},{5,133},{133,1},{2... | collective-permute-start | bytes 786440 | tf_op jit(solution)/shard_map/ppermute | solution.py:360
  228.9 13.2 %collective-permute-start.20 = (bf16[64,2048]{1,0:T(8,128)(2,1)S(1)}, bf16[64,2048]{1,0:T(8,128)(2,1)S(1)}, u32[]{:S(2)}, u32[]{:S(2)}) collective-permute-start(bf16[64,2048]{1,0:T(8,128)(2,1)S(1)} %join.1), channel_id=1, source_target_pairs={{128,0},{4,128},{132,4},{0,132},{129,1},{5,129},{133,5},{1,133},{1... | collective-permute-start | bytes 786440 | tf_op jit(solution)/shard_map/ppermute | solution.py:356
  (10 other events, 13.8 us)

commit v3 on v1

v3 whole, which is shorter than its diff:
```python
import functools
import jax
import jax.numpy as jnp
from jax import lax
from jax.sharding import Mesh, PartitionSpec as P
from jax.experimental import pallas as pl
from jax.experimental.pallas import tpu as pltpu

SLOTS = 12
EARLY = 4
LATE = SLOTS - EARLY
DESTS = 16
TOP = 8
BF = jnp.bfloat16
SMEM = pl.BlockSpec(memory_space=pltpu.SMEM)
VMEM = pl.BlockSpec(memory_space=pltpu.VMEM)
ANY = pl.BlockSpec(memory_space=pl.ANY)


def grant(mib):
    return pltpu.CompilerParams(vmem_limit_bytes=mib << 20)


def pack_kernel(t_ref, r_ref, w_ref, o_ref):
    half = t_ref.shape[0] // 2
    tok = t_ref.shape[0]
    o_ref[0:half, :] = t_ref[0:half, :]
    o_ref[half + TOP :, :] = t_ref[half:, :]
    weight = w_ref[...]
    high = weight // 256
    low = weight - high * 256
    gap = jnp.zeros((TOP, 128 - tok), jnp.float32)
    parts = []
    for v in (r_ref[...], high, low):
        parts += [v.astype(jnp.float32), gap]
    used = 128 * 3
    o_ref[half : half + TOP, 0:used] = jnp.concatenate(parts, axis=1).astype(BF)
    o_ref[half : half + TOP, used:] = jnp.zeros((TOP, t_ref.shape[1] - used), BF)


def weights_kernel(s_ref, g_ref, u_ref, d_ref, mgu, ogu, md, od, bgu, bd, sem_in, sem_out):
    zp = s_ref[0]
    loads, stores = [], []
    for which in (0, 1):
        e = zp if which == 0 else 1 - zp
        gu_out, d_out = ((mgu, md), (ogu, od))[which]
        for i, src in enumerate((g_ref, u_ref)):
            loads.append(pltpu.make_async_copy(src.at[e], bgu.at[which, i], sem_in.at[which * 3 + i]))
            stores.append(
                pltpu.make_async_copy(bgu.at[which, i], gu_out.at[i], sem_out.at[which * 3 + i])
            )
        loads.append(pltpu.make_async_copy(d_ref.at[e], bd.at[which], sem_in.at[which * 3 + 2]))
        stores.append(pltpu.make_async_copy(bd.at[which], d_out, sem_out.at[which * 3 + 2]))
    for c in loads:
        c.start()
    for a, b in zip(loads, stores):
        a.wait()
        b.start()
    for b in stores:
        b.wait()


def read_meta(ref, half, tok):
    rows = ref[half : half + TOP, 0:384].astype(jnp.float32)
    return rows[:, 0:tok], rows[:, 128 : 128 + tok] * 256.0 + rows[:, 256 : 256 + tok]


def plane_experts(s_ref, cap_ref, hot_ref, tok):
    base = s_ref[1]
    row = lax.broadcasted_iota(jnp.int32, (DESTS, tok), 0)
    expert = (row // 4) * 16 + (row % 4) * 2 + base
    limit = jnp.zeros((DESTS, tok), jnp.int32)
    for d in range(DESTS):
        e = (d // 4) * 16 + (d % 4) * 2 + base
        cap = jnp.where(e == hot_ref[0], SLOTS, cap_ref[e])
        limit = jnp.where(row == d, cap, limit)
    return expert.astype(jnp.float32), limit.astype(jnp.float32)


def slots_of(named_by, expert, limit, first, tok, turn=0):
    earlier = jnp.where(
        lax.broadcasted_iota(jnp.int32, (tok, tok), 0) < lax.broadcasted_iota(jnp.int32, (tok, tok), 1),
        1.0,
        0.0,
    ).astype(BF)
    named = named_by[0:1, :] == expert
    for k in range(1, TOP):
        named = jnp.logical_or(named, named_by[k : k + 1, :] == expert)
    rank = jnp.dot(jnp.where(named, 1.0, 0.0).astype(BF), earlier, preferred_element_type=jnp.float32)
    kept = jnp.logical_and(named, rank < limit)
    if turn:
        rank = jnp.where(rank < turn, rank + (SLOTS - turn), rank - turn)
    return jnp.where(kept, rank + first, -1.0).astype(jnp.int32)


def match_rows(slots, per, width):
    want = lax.broadcasted_iota(jnp.int32, (DESTS, per, width), 1)
    return want == slots[:, None, :]


def dispatch_kernel(far, s_ref, cap_ref, hot_ref, *refs):
    blocks = 3 if far else 2
    o_ref, factor_refs = refs[blocks], refs[blocks + 1 :]
    refs = refs[:blocks]
    half = 32
    tok = 2 * half
    per = o_ref.shape[1]
    expert, limit = plane_experts(s_ref, cap_ref, hot_ref, tok)
    slots, shares = [], []
    for b, ref in enumerate(refs[:2]):
        routes, weight = read_meta(ref, half, tok)
        turn = EARLY if b == 0 and not far else 0
        slots.append(slots_of(routes, expert, limit, b * SLOTS, tok, turn))
        share = weight / jnp.sum(weight, axis=0, keepdims=True)
        picked = jnp.zeros((DESTS, tok), jnp.float32)
        for k in range(TOP):
            picked = picked + jnp.where(routes[k : k + 1, :] == expert, share[k : k + 1, :], 0.0)
        shares.append(picked)
    slots = jnp.concatenate(slots, axis=1)
    shares = jnp.concatenate(shares, axis=1)
    match = match_rows(slots, per, 2 * tok)
    chosen = jnp.where(match, 1.0, 0.0).reshape(DESTS * per, 2 * tok).astype(BF)
    factor = jnp.where(match, shares[:, None, :], 0.0)
    if far:
        pieces = [factor]
    else:
        pieces = [factor[:, LATE:, :], factor[:, 0:LATE, 0:tok]]
    for piece, f_ref in zip(pieces, factor_refs):
        piece = piece.reshape(-1, piece.shape[2]).T
        high = piece.astype(BF)
        f_ref[0] = high
        f_ref[1] = (piece - high.astype(jnp.float32)).astype(BF)
    width = o_ref.shape[2]
    step = 512
    for n in range(0, width, step):
        at = slice(n, n + step)
        rows = []
        for b, ref in enumerate(refs[:2]):
            rows.append(ref[0:half, at])
            if far and b == 1:
                rows.append(refs[2][:, at])
            else:
                rows.append(ref[half + TOP :, at])
        got = jnp.dot(chosen, jnp.concatenate(rows, axis=0), preferred_element_type=jnp.float32)
        o_ref[:, :, at] = got.astype(BF).reshape(DESTS, per, step)


def weighted(f_ref, rows):
    part = jnp.dot(f_ref[0], rows, preferred_element_type=jnp.float32)
    return part + jnp.dot(f_ref[1], rows, preferred_element_type=jnp.float32)


def combine_a_kernel(fb_ref, fa_ref, r_ref, own, c_top, c_low, a_top, a_low, b_top, b_low):
    half = 32
    width = r_ref.shape[2]
    near = 2 * SLOTS - LATE
    step = 512
    for n in range(0, width, step):
        at = slice(n, n + step)
        part = weighted(fb_ref, r_ref[:, 0:near, at].reshape(DESTS * near, step))
        own[:, at] = part[0 : 2 * half]
        c_top[:, at] = part[2 * half : 3 * half].astype(c_top.dtype)
        c_low[:, at] = part[3 * half :].astype(c_low.dtype)
        part = weighted(fa_ref, r_ref[:, near:, at].reshape(DESTS * 2 * SLOTS, step))
        for i, o in enumerate((a_top, a_low, b_top, b_low)):
            o[:, at] = part[i * half : (i + 1) * half].astype(o.dtype)


def combine_b_kernel(f_ref, r_ref, own_ref, out_ref):
    width = r_ref.shape[2]
    step = 512
    for n in range(0, width, step):
        at = slice(n, n + step)
        out_ref[:, at] = own_ref[:, at] + weighted(f_ref, r_ref[:, :, at].reshape(DESTS * LATE, step))


def join_kernel(at_top, one_ref, two_ref, over_ref, out_ref):
    half = over_ref.shape[0]
    total = (one_ref[...] + over_ref[...].astype(jnp.float32)).astype(BF)
    out_ref[0:half, :] = total if at_top else two_ref[...]
    out_ref[half:, :] = two_ref[...] if at_top else total


def up_kernel(off_ref, xa_ref, xb_ref, *refs):
    groups = refs[0:8]
    ha_ref, hn_ref, hl_ref, wg, wu, gate_s, sems = refs[8:]
    size = groups[0].shape[1]
    copies = [[], []]
    for which, dst in enumerate((wg, wu)):
        for i in range(8):
            at = pl.multiple_of(off_ref[i] * size, size)
            copies[which].append(
                pltpu.make_async_copy(
                    groups[i].at[which], dst.at[pl.ds(at, size), :], sems.at[which * 8 + i]
                )
            )
    for group in copies:
        for c in group:
            c.start()
    rows = xa_ref.shape[0]
    part = 8
    per = 2 * SLOTS
    step = part * per
    for c in copies[0]:
        c.wait()
    for j, x_ref in enumerate((xa_ref, xb_ref)):
        for r in range(0, rows, step):
            gate_s[j * rows + r : j * rows + r + step, :] = jnp.dot(
                x_ref[r : r + step, :], wg[...], preferred_element_type=jnp.float32
            )
    for c in copies[1]:
        c.wait()
    for j, x_ref in enumerate((xa_ref, xb_ref)):
        for k, r in enumerate(range(0, rows, step)):
            gate = gate_s[j * rows + r : j * rows + r + step, :]
            up = jnp.dot(x_ref[r : r + step, :], wu[...], preferred_element_type=jnp.float32)
            hidden = gate / (1.0 + jnp.exp(-gate)) * up
            if j == 0:
                ha_ref[r : r + step, :] = hidden.astype(BF)
            else:
                hidden = hidden.reshape(part, per, hidden.shape[1])
                near = part * (per - LATE)
                hn_ref[k * near : (k + 1) * near, :] = (
                    hidden[:, LATE:, :].reshape(near, hidden.shape[2]).astype(BF)
                )
                late = part * LATE
                hl_ref[k * late : (k + 1) * late, :] = (
                    hidden[:, 0:LATE, :].reshape(late, hidden.shape[2]).astype(BF)
                )


def down_kernel(count, off_ref, *refs):
    h_refs = refs[0:count]
    downs = refs[count : count + 8]
    o_ref, wd, done, sems, out_sems = refs[count + 8 :]
    size = downs[0].shape[1]
    outs = []
    copies = [pltpu.make_async_copy(downs[i], wd.at[i], sems.at[i]) for i in range(8)]
    for c in copies:
        c.start()
    part = 8
    for i in range(8):
        copies[i].wait()
        at = pl.ds(pl.multiple_of(off_ref[i] * size, size), size)
        first = 0
        for h_ref in h_refs:
            per = h_ref.shape[0] // DESTS
            for d in range(0, DESTS, part):
                got = jnp.dot(
                    h_ref[d * per : (d + part) * per, :], wd[i], preferred_element_type=jnp.float32
                )
                done[i, d : d + part, first : first + per, :] = got.reshape(part, per, size).astype(BF)
            first += per
        outs.append(pltpu.make_async_copy(done.at[i], o_ref.at[:, :, at], out_sems.at[i]))
        outs[i].start()
    for c in outs:
        c.wait()


def cost(flops, moved, hard=0):
    return pl.CostEstimate(flops=flops, bytes_accessed=moved, transcendentals=hard)


def shape(dims, kind=BF):
    return jax.ShapeDtypeStruct(dims, kind)


def exchange(value):
    return lax.all_to_all(value, ("x", "y"), split_axis=0, concat_axis=0, tiled=True)


def per_device(tokens, routes, route_weight, capacity, hot_expert, w_gate, w_up, w_down):
    zp, zq, core, zh = (lax.axis_index(n) for n in ("zp", "zq", "core", "zh"))
    ring = ("zp", "zh")
    order = [0, 2, 1, 3]
    fwd = [(order[i], order[(i + 1) % 4]) for i in range(4)]
    back = [(order[(i + 1) % 4], order[i]) for i in range(4)]
    swap = [(0, 1), (1, 0)]
    tok, width = tokens.shape
    half = tok // 2
    ff = w_gate.shape[2]
    piece = w_gate.shape[1]
    per = 2 * SLOTS
    rows = DESTS * per
    split = half + TOP

    scal = jnp.stack([zp, zh * 8 + zp]).astype(jnp.int32)
    own = pl.pallas_call(
        pack_kernel,
        out_shape=shape((tok + TOP, width)),
        in_specs=[VMEM] * 3,
        out_specs=VMEM,
        compiler_params=grant(8),
        cost_estimate=cost(0, 600 << 10),
        name="pack",
    )(tokens, routes.T, route_weight.T)
    tok3 = lax.ppermute(own, ring, back)
    tok1 = lax.ppermute(own, ring, fwd)
    mine_gu, other_gu, mine_d, other_d = pl.pallas_call(
        weights_kernel,
        out_shape=[shape((2, piece, ff)), shape((2, piece, ff)), shape((ff, piece)), shape((ff, piece))],
        in_specs=[SMEM, ANY, ANY, ANY],
        out_specs=[ANY] * 4,
        scratch_shapes=[
            pltpu.VMEM((2, 2, piece, ff), BF),
            pltpu.VMEM((2, ff, piece), BF),
            pltpu.SemaphoreType.DMA((6,)),
            pltpu.SemaphoreType.DMA((6,)),
        ],
        compiler_params=grant(56),
        cost_estimate=cost(0, 5 << 20),
        name="pack_weights",
    )(scal, w_gate, w_up, w_down)

    def shards(mine, other):
        a = lax.ppermute(other, "zp", swap)
        b = lax.ppermute(mine, "zq", swap)
        c = lax.ppermute(a, "zq", swap)
        near = [lax.ppermute(v, "core", swap) for v in (mine, a, b, c)]
        return [mine, a, b, c] + near

    gates_ups = shards(mine_gu, other_gu)
    downs = shards(mine_d, other_d)

    far_top = lax.ppermute(tok1[:split], ring, fwd)
    far_low = lax.ppermute(tok3[split:], ring, back)

    near = per - LATE

    def dispatch(factor_shapes, *blocks):
        return pl.pallas_call(
            functools.partial(dispatch_kernel, len(blocks) == 3),
            out_shape=[shape((DESTS, per, width))] + [shape((2,) + f) for f in factor_shapes],
            in_specs=[SMEM] * 3 + [VMEM] * len(blocks),
            out_specs=[VMEM] * (1 + len(factor_shapes)),
            compiler_params=grant(12),
            cost_estimate=cost(2 * rows * 2 * tok * width, 2 << 20),
        )(scal, capacity, hot_expert, *blocks)

    sent_b, fac_near, fac_late = dispatch([(2 * tok, DESTS * near), (tok, DESTS * LATE)], own, tok3)
    x_b = exchange(sent_b).reshape(rows, width)
    sent_a, fac_a = dispatch([(2 * tok, rows)], tok1, far_top, far_low)
    x_a = exchange(sent_a).reshape(rows, width)

    place = []
    for g in (0, 1):
        for b in (0, 1):
            for a in (0, 1):
                place.append((zp ^ a) * 4 + (zq ^ b) * 2 + (core ^ g))
    off = jnp.stack(place).astype(jnp.int32)
    h_a, h_near, h_late = pl.pallas_call(
        up_kernel,
        out_shape=[shape((n, ff)) for n in (rows, DESTS * near, DESTS * LATE)],
        in_specs=[SMEM, VMEM, VMEM] + [ANY] * 8,
        out_specs=[VMEM] * 3,
        scratch_shapes=[pltpu.VMEM((width, ff), BF)] * 2
        + [pltpu.VMEM((2 * rows, ff), jnp.float32), pltpu.SemaphoreType.DMA((16,))],
        compiler_params=grant(24),
        cost_estimate=cost(8 * rows * width * ff, 11 << 20, 2 * rows * ff),
        name="gate_up",
    )(off, x_a, x_b, *gates_ups)

    def down(*hs):
        count = sum(h.shape[0] for h in hs)
        return pl.pallas_call(
            functools.partial(down_kernel, len(hs)),
            out_shape=shape((DESTS, count // DESTS, width)),
            in_specs=[SMEM] + [VMEM] * len(hs) + [ANY] * 8,
            out_specs=ANY,
            scratch_shapes=[
                pltpu.VMEM((8, ff, piece), BF),
                pltpu.VMEM((8, DESTS, count // DESTS, piece), BF),
                pltpu.SemaphoreType.DMA((8,)),
                pltpu.SemaphoreType.DMA((8,)),
            ],
            compiler_params=grant(54),
            cost_estimate=cost(2 * count * width * ff, 6 << 20),
        )(off, *hs, *downs)

    def local(kernel, ins, outs, mib):
        return pl.pallas_call(
            kernel,
            out_shape=outs,
            in_specs=[VMEM] * len(ins),
            out_specs=[VMEM] * len(outs),
            compiler_params=grant(mib),
            cost_estimate=cost(1 << 20, 3 << 20),
        )(*ins)

    f32 = jnp.float32
    back_a = exchange(down(h_near, h_a))
    back_b = exchange(down(h_late))
    part0, p3_top, p3_low, p1_top, p1_low, p2_top, p2_low = local(
        combine_a_kernel,
        (fac_near, fac_a, back_a),
        [shape((tok, width), f32)] + [shape((half, width), k) for k in (BF, f32, f32, BF, BF, BF)],
        10,
    )
    over_back = lax.ppermute(p2_top, ring, back)
    over_fwd = lax.ppermute(p2_low, ring, fwd)
    block = [shape((tok, width))]
    (to_back,) = local(functools.partial(join_kernel, True), (p1_top, p1_low, over_back), block, 56)
    from_next = lax.ppermute(to_back, ring, back)
    (to_fwd,) = local(functools.partial(join_kernel, False), (p3_low, p3_top, over_fwd), block, 56)
    from_prev = lax.ppermute(to_fwd, ring, fwd)
    (part0,) = local(combine_b_kernel, (fac_late, back_b, part0), [shape((tok, width), f32)], 6)
    total = part0 + from_next.astype(f32) + from_prev.astype(f32)
    return total.astype(BF)


def solution(mesh):
    fine = Mesh(mesh.devices.reshape(2, 2, 2, 4, 2, 4), ("zp", "zq", "core", "x", "zh", "y"))
    dp, ex = ("zp", "zq", "core"), ("x", "zh", "y")
    in_specs = (
        P(dp + ex, None),
        P(dp + ex, None),
        P(dp + ex, None),
        P(),
        P(),
        P(ex, dp, None),
        P(ex, dp, None),
        P(ex, None, dp),
    )

    return jax.shard_map(
        per_device, mesh=fine, in_specs=in_specs, out_specs=P(dp + ex, None), check_vma=False
    )
```

time: 253 us -> 258 us (1.020)
  the two profiles are of different devices: /device:TPU:32 before, /device:TPU:37 now
where the time goes in v3:
time: 258 us; the launch traced here: 255 us
  waiting for transfers between devices  137 us (53%)
  starting transfers between devices  72.8 us (28%)
  Pallas kernels  31.2 us (12%)
  local copies, waits for them, and re-layouts  12.4 us (5%)
    ppermute x1, waiting for transfers between devices, per_device(): tok1 = lax.ppermute(own, ring, fwd)  46.1 us
    all_to_all x4, waiting for transfers between devices, exchange(): lax.all_to_all(value, ('x', 'y'), split_axis=0, concat_axis=0, tiled=True)  28.9 us
    all_to_all x4, starting transfers between devices, exchange(): lax.all_to_all(value, ('x', 'y'), split_axis=0, concat_axis=0, tiled=True)  28.8 us
    ppermute x2, waiting for transfers between devices, shards(): a = lax.ppermute(other, 'zp', swap)  23 us
    ppermute x8, starting transfers between devices, shards(): near = [lax.ppermute(v, 'core', swap) for v in (mine, a, b, c)]  17.1 us
    unnamed x42, local copies, waits for them, and re-layouts  12.3 us
    pallas_call x2, Pallas kernels, down(): pl.pallas_call(functools.partial(down_kernel, len(hs)), out_shape=shape((...  11.3 us
    ppermute x1, waiting for transfers between devices, per_device(): tok3 = lax.ppermute(own, ring, back)  10.6 us
  transfers between devices with their start and end apart: 26, of which 11 were waited for; matrix products, arithmetic and copies ran while one was open for 0% of the time, Pallas kernels for 9%

profile of v3, /device:TPU:37, one launch (start us, length us, event | category | flops | bytes accessed | tf_op | source)
XLA Modules:
  0.0 254.6 jit_solution(9490301957502393261)
XLA Ops:
  2.4 5.2 %collective-permute-start = (bf16[72,2048]{1,0:T(8,128)(2,1)S(1)}, bf16[72,2048]{1,0:T(8,128)(2,1)S(1)}, u32[]{:S(2)}, u32[]{:S(2)}) collective-permute-start(bf16[72,2048]{1,0:T(8,128)(2,1)S(1)} %pack.1.refs_0_), channel_id=1, source_target_pairs={{128,0},{4,128},{132,4},{0,132},{129,1},{5,129},{133,5},{1,133},{1... | collective-permute-start | bytes 884744 | tf_op jit(solution)/shard_map/ppermute | solution.py:297
  8.3 10.6 %collective-permute-done.refs_1_ = bf16[72,2048]{1,0:T(8,128)(2,1)S(1)} collective-permute-done((bf16[72,2048]{1,0:T(8,128)(2,1)S(1)}, bf16[72,2048]{1,0:T(8,128)(2,1)S(1)}, u32[]{:S(2)}, u32[]{:S(2)}) %collective-permute-start) | collective-permute-done | bytes 294944 | tf_op jit(solution)/shard_map/ppermute | solution.py:297
  19.5 2.5 shard_map.82
  22.0 6.9 %all-to-all-start.1 = ((bf16[16,24,2048]{2,1,0:T(8,128)(2,1)}), bf16[16,24,2048]{2,1,0:T(8,128)(2,1)S(1)}, u32[]{:S(2)}, u32[]{:S(2)}) async-start(bf16[16,24,2048]{2,1,0:T(8,128)(2,1)} %get-tuple-element.26), calls=%async_computation.1 | async-start | bytes 3145728 | tf_op jit(solution)/shard_map/all_to_all | solution.py:269
  28.9 3.4 %pack_weights.1 = (bf16[2,256,768]{2,1,0:T(8,128)(2,1)}, bf16[2,256,768]{2,1,0:T(8,128)(2,1)}, bf16[768,256]{1,0:T(8,128)(2,1)}, bf16[768,256]{1,0:T(8,128)(2,1)}) custom-call(s32[2]{0:T(128)} %copy-done.12, bf16[2,256,768]{2,1,0:T(8,128)(2,1)} %g_ref.1, bf16[2,256,768]{2,1,0:T(8,128)(2,1)} %u_ref.1, bf16[2,768,256]{2,1,0:T(8,128)(2,1)} %d_ref.1), custom_call_target="tpu_custom_call" | custom-call | bytes 5242880 | tf_op jit(solution)/shard_map/pack_weights/pallas_call | solution.py:299
  32.4 2.4 collective-permute-start.1
  34.7 46.1 %collective-permute-done.1.refs_0_ = bf16[72,2048]{1,0:T(8,128)(2,1)S(1)} collective-permute-done((bf16[72,2048]{1,0:T(8,128)(2,1)S(1)}, bf16[72,2048]{1,0:T(8,128)(2,1)S(1)}, u32[]{:S(2)}, u32[]{:S(2)}) %collective-permute-start.1) | collective-permute-done | bytes 294944 | tf_op jit(solution)/shard_map/ppermute | solution.py:298
  80.8 3.2 %collective-permute-start.2 = (bf16[40,2048]{1,0:T(8,128)(2,1)S(1)}, bf16[40,2048]{1,0:T(8,128)(2,1)S(1)}, u32[]{:S(2)}, u32[]{:S(2)}) collective-permute-start(bf16[40,2048]{1,0:T(8,128)(2,1)S(1)} %slice.8), channel_id=1, source_target_pairs={{0,128},{128,4},{4,132},{132,0},{1,129},{129,5},{5,133},{133,1},{2... | collective-permute-start | bytes 491528 | tf_op jit(solution)/shard_map/ppermute | solution.py:325
  84.0 5.0 %collective-permute-start.3 = (bf16[32,2048]{1,0:T(8,128)(2,1)S(1)}, bf16[32,2048]{1,0:T(8,128)(2,1)S(1)}, u32[]{:S(2)}, u32[]{:S(2)}) collective-permute-start(bf16[32,2048]{1,0:T(8,128)(2,1)S(1)} %slice.9), channel_id=1, source_target_pairs={{128,0},{4,128},{132,4},{0,132},{129,1},{5,129},{133,5},{1,133},{1... | collective-permute-start | bytes 393224 | tf_op jit(solution)/shard_map/ppermute | solution.py:326
  89.0 1.5 collective-permute-start.6
  94.1 6.7 %all-to-all-start = ((bf16[16,24,2048]{2,1,0:T(8,128)(2,1)}), bf16[16,24,2048]{2,1,0:T(8,128)(2,1)S(1)}, u32[]{:S(2)}, u32[]{:S(2)}) async-start(bf16[16,24,2048]{2,1,0:T(8,128)(2,1)} %copy-done), calls=%async_computation | async-start | bytes 3145728 | tf_op jit(solution)/shard_map/all_to_all | solution.py:269
  100.8 2.6 %collective-permute-start.11 = (bf16[768,256]{1,0:T(8,128)(2,1)}, bf16[768,256]{1,0:T(8,128)(2,1)}, u32[]{:S(2)}, u32[]{:S(2)}) collective-permute-start(bf16[768,256]{1,0:T(8,128)(2,1)} %get-tuple-element.31), channel_id=1, source_target_pairs={{0,128},{128,0},{1,129},{129,1},{2,130},{130,2},{3,131},{131,3},{4... | collective-permute-start | bytes 1179656 | tf_op jit(solution)/shard_map/ppermute | solution.py:316
  103.3 5.7 %collective-permute-start.7 = (bf16[2,256,768]{2,1,0:T(8,128)(2,1)}, bf16[2,256,768]{2,1,0:T(8,128)(2,1)}, u32[]{:S(2)}, u32[]{:S(2)}) collective-permute-start(bf16[2,256,768]{2,1,0:T(8,128)(2,1)} %get-tuple-element.27.refs_0_), channel_id=1, source_target_pairs={{0,32},{32,0},{1,33},{33,1},{2,34},{34,2},{3,35},{35,3},{4,36},{36... | collective-permute-start | bytes 2359304 | tf_op jit(solution)/shard_map/ppermute | solution.py:319
  109.1 23.0 %collective-permute-done.11.refs_2_.refs_3_ = bf16[768,256]{1,0:T(8,128)(2,1)} collective-permute-done((bf16[768,256]{1,0:T(8,128)(2,1)}, bf16[768,256]{1,0:T(8,128)(2,1)}, u32[]{:S(2)}, u32[]{:S(2)}) %collective-permute-start.11) | collective-permute-done | bytes 393248 | tf_op jit(solution)/shard_map/ppermute | solution.py:316
  132.0 5.4 %collective-permute-start.8 = (bf16[2,256,768]{2,1,0:T(8,128)(2,1)}, bf16[2,256,768]{2,1,0:T(8,128)(2,1)}, u32[]{:S(2)}, u32[]{:S(2)}) collective-permute-start(bf16[2,256,768]{2,1,0:T(8,128)(2,1)} %collective-permute-done.4.refs_1_), channel_id=1, source_target_pairs={{0,32},{32,0},{1,33},{33,1},{2,34},{34,2},{3,35},{35,3},{4,36},{36... | collective-permute-start | bytes 2359304 | tf_op jit(solution)/shard_map/ppermute | solution.py:319
  138.0 5.3 %collective-permute-done.12.refs_3_.refs_4_ = bf16[768,256]{1,0:T(8,128)(2,1)} collective-permute-done((bf16[768,256]{1,0:T(8,128)(2,1)}, bf16[768,256]{1,0:T(8,128)(2,1)}, u32[]{:S(2)}, u32[]{:S(2)}) %collective-permute-start.12) | collective-permute-done | bytes 393248 | tf_op jit(solution)/shard_map/ppermute | solution.py:317
  143.4 2.6 %collective-permute-start.14 = (bf16[768,256]{1,0:T(8,128)(2,1)}, bf16[768,256]{1,0:T(8,128)(2,1)}, u32[]{:S(2)}, u32[]{:S(2)}) collective-permute-start(bf16[768,256]{1,0:T(8,128)(2,1)} %get-tuple-element.30.refs_1_.refs_2_), channel_id=1, source_target_pairs={{0,32},{32,0},{1,33},{33,1},{2,34},{34,2},{3,35},{35,3},{4,36},{36... | collective-permute-start | bytes 1179656 | tf_op jit(solution)/shard_map/ppermute | solution.py:319
  146.0 6.8 %collective-permute-done.13.refs_4_.refs_5_ = bf16[768,256]{1,0:T(8,128)(2,1)} collective-permute-done((bf16[768,256]{1,0:T(8,128)(2,1)}, bf16[768,256]{1,0:T(8,128)(2,1)}, u32[]{:S(2)}, u32[]{:S(2)}) %collective-permute-start.13) | collective-permute-done | bytes 393248 | tf_op jit(solution)/shard_map/ppermute | solution.py:318
  152.9 2.3 collective-permute-start.15
  156.8 7.8 %gate_up.1 = (bf16[384,768]{1,0:T(8,128)(2,1)S(1)}, bf16[256,768]{1,0:T(8,128)(2,1)S(1)}, bf16[128,768]{1,0:T(8,128)(2,1)S(1)}) custom-call(s32[8]{0:T(128)S(1)} %stack.47.off_ref, bf16[384,2048]{1,0:T(8,128)(2,1)S(1)} %bitcast.15, bf16[384,2048]{1,0:T(8,128)(2,1)S(1)} %bitcast.14, bf16[2,256,768]{2,1,0:T(8,128)(2,1)S(1)} %copy-done.14, ...), custom_call_target="tpu_custom_call" | custom-call | flops 4831838208 | bytes 11534336 | tf_op jit(solution)/shard_map/gate_up/pallas_call | solution.py:351
  166.9 6.5 %shard_map.85 = bf16[16,40,2048]{2,1,0:T(8,128)(2,1)} custom-call(s32[8]{0:T(128)} %copy-done.11, bf16[256,768]{1,0:T(8,128)(2,1)} %copy-done.18, bf16[384,768]{1,0:T(8,128)(2,1)} %copy-done.17, bf16[768,256]{1,0:T(8,128)(2,1)} %get-tuple-element.30.refs_1_.refs_2_, bf16[768,256]{1,0:T(8,128)(2,1)} %collective-permute-done.11.refs_2_.refs_3_, ...), custom_call_target="tpu_custom_call" | custom-call | flops 2013265920 | bytes 6291456 | tf_op jit(solution)/shard_map/pallas_call | solution.py:365
  173.5 6.7 %all-to-all-start.3 = ((bf16[16,40,2048]{2,1,0:T(8,128)(2,1)}), bf16[16,40,2048]{2,1,0:T(8,128)(2,1)S(1)}, u32[]{:S(2)}, u32[]{:S(2)}) async-start(bf16[16,40,2048]{2,1,0:T(8,128)(2,1)} %shard_map.85), calls=%async_computation.3 | async-start | bytes 5242880 | tf_op jit(solution)/shard_map/all_to_all | solution.py:269
  180.1 4.8 %shard_map.84 = bf16[16,8,2048]{2,1,0:T(8,128)(2,1)} custom-call(s32[8]{0:T(128)} %copy-done.11, bf16[128,768]{1,0:T(8,128)(2,1)} %copy-done.6, bf16[768,256]{1,0:T(8,128)(2,1)} %get-tuple-element.30.refs_1_.refs_2_, bf16[768,256]{1,0:T(8,128)(2,1)} %collective-permute-done.11.refs_2_.refs_3_, bf16[768,256]{1,0:T(8,128)(2,1)} %collective-permute-done.12.refs_3_.refs_4_, ...), custom_call_target="tpu_custom_call" | custom-call | flops 402653184 | bytes 6291456 | tf_op jit(solution)/shard_map/pallas_call | solution.py:365
  184.9 28.9 %all-to-all-done.3.r_ref = bf16[16,40,2048]{2,1,0:T(8,128)(2,1)S(1)} async-done(((bf16[16,40,2048]{2,1,0:T(8,128)(2,1)}), bf16[16,40,2048]{2,1,0:T(8,128)(2,1)S(1)}, u32[]{:S(2)}, u32[]{:S(2)}) %all-to-all-start.3) | async-done | bytes 2621472 | tf_op jit(solution)/shard_map/all_to_all | solution.py:269
  213.9 8.5 %all-to-all-start.2 = ((bf16[16,8,2048]{2,1,0:T(8,128)(2,1)}), bf16[16,8,2048]{2,1,0:T(8,128)(2,1)S(1)}, u32[]{:S(2)}, u32[]{:S(2)}) async-start(bf16[16,8,2048]{2,1,0:T(8,128)(2,1)} %shard_map.84), calls=%async_computation.2 | async-start | bytes 1048576 | tf_op jit(solution)/shard_map/all_to_all | solution.py:269
  226.9 3.6 %collective-permute-start.18 = (bf16[32,2048]{1,0:T(8,128)(2,1)S(1)}, bf16[32,2048]{1,0:T(8,128)(2,1)S(1)}, u32[]{:S(2)}, u32[]{:S(2)}) collective-permute-start(bf16[32,2048]{1,0:T(8,128)(2,1)S(1)} %get-tuple-element.39), channel_id=1, source_target_pairs={{128,0},{4,128},{132,4},{0,132},{129,1},{5,129},{133,5},{1,133},{1... | collective-permute-start | bytes 393224 | tf_op jit(solution)/shard_map/ppermute | solution.py:399
  230.5 4.8 %collective-permute-done.20.over_ref = bf16[32,2048]{1,0:T(8,128)(2,1)S(1)} collective-permute-done((bf16[32,2048]{1,0:T(8,128)(2,1)S(1)}, bf16[32,2048]{1,0:T(8,128)(2,1)S(1)}, u32[]{:S(2)}, u32[]{:S(2)}) %collective-permute-start.20) | collective-permute-done | bytes 131104 | tf_op jit(solution)/shard_map/ppermute | solution.py:400
  235.9 1.8 shard_map.89
  238.4 1.8 shard_map.88
  240.1 3.5 %collective-permute-start.19 = (bf16[64,2048]{1,0:T(8,128)(2,1)}, bf16[64,2048]{1,0:T(8,128)(2,1)S(1)}, u32[]{:S(2)}, u32[]{:S(2)}) collective-permute-start(bf16[64,2048]{1,0:T(8,128)(2,1)} %shard_map.88), channel_id=1, source_target_pairs={{128,0},{4,128},{132,4},{0,132},{129,1},{5,129},{133,5},{1,133},{1... | collective-permute-start | bytes 786440 | tf_op jit(solution)/shard_map/ppermute | solution.py:403
  244.0 4.0 %collective-permute-done.21 = bf16[64,2048]{1,0:T(8,128)(2,1)S(1)} collective-permute-done((bf16[64,2048]{1,0:T(8,128)(2,1)}, bf16[64,2048]{1,0:T(8,128)(2,1)S(1)}, u32[]{:S(2)}, u32[]{:S(2)}) %collective-permute-start.21) | collective-permute-done | bytes 262176 | tf_op jit(solution)/shard_map/ppermute | solution.py:405
  248.0 5.9 %collective-permute-done.19 = bf16[64,2048]{1,0:T(8,128)(2,1)S(1)} collective-permute-done((bf16[64,2048]{1,0:T(8,128)(2,1)}, bf16[64,2048]{1,0:T(8,128)(2,1)S(1)}, u32[]{:S(2)}, u32[]{:S(2)}) %collective-permute-start.19) | collective-permute-done | bytes 262176 | tf_op jit(solution)/shard_map/ppermute | solution.py:403
  (78 shorter events, 18.2 us)
Async XLA Ops:
  2.4 16.5 %collective-permute-start = (bf16[72,2048]{1,0:T(8,128)(2,1)S(1)}, bf16[72,2048]{1,0:T(8,128)(2,1)S(1)}, u32[]{:S(2)}, u32[]{:S(2)}) collective-permute-start(bf16[72,2048]{1,0:T(8,128)(2,1)S(1)} %pack.1.refs_0_), channel_id=1, source_target_pairs={{128,0},{4,128},{132,4},{0,132},{129,1},{5,129},{133,5},{1,133},{1... | collective-permute-start | bytes 884744 | tf_op jit(solution)/shard_map/ppermute | solution.py:297
  8.3 13.7 %copy-start.12 = (s32[2]{0:T(128)}, s32[2]{0:T(128)S(1)}, u32[]{:S(2)}) copy-start(s32[2]{0:T(128)S(1)} %pad_add_fusion.s_ref) | copy-start | bytes 28
  22.0 72.1 %all-to-all-start.1 = ((bf16[16,24,2048]{2,1,0:T(8,128)(2,1)}), bf16[16,24,2048]{2,1,0:T(8,128)(2,1)S(1)}, u32[]{:S(2)}, u32[]{:S(2)}) async-start(bf16[16,24,2048]{2,1,0:T(8,128)(2,1)} %get-tuple-element.26), calls=%async_computation.1 | async-start | bytes 3145728 | tf_op jit(solution)/shard_map/all_to_all | solution.py:269
  28.9 62.7 %copy-start.13 = (s32[2]{0:T(128)S(1)}, s32[2]{0:T(128)}, u32[]{:S(2)}) copy-start(s32[2]{0:T(128)} %copy-done.12) | copy-start | bytes 28
  28.9 62.7 %copy-start.16 = (s32[64]{0:T(128)S(1)}, s32[64]{0:T(128)}, u32[]{:S(2)}) copy-start(s32[64]{0:T(128)} %cap_ref.3) | copy-start | bytes 772
  32.3 56.7 %collective-permute-start.4 = (bf16[2,256,768]{2,1,0:T(8,128)(2,1)}, bf16[2,256,768]{2,1,0:T(8,128)(2,1)}, u32[]{:S(2)}, u32[]{:S(2)}) collective-permute-start(bf16[2,256,768]{2,1,0:T(8,128)(2,1)} %get-tuple-element.28), channel_id=1, source_target_pairs={{0,128},{128,0},{1,129},{129,1},{2,130},{130,2},{3,131},{131,3},{4... | collective-permute-start | bytes 2359304 | tf_op jit(solution)/shard_map/ppermute | solution.py:316
  32.4 48.4 %collective-permute-start.1 = (bf16[72,2048]{1,0:T(8,128)(2,1)S(1)}, bf16[72,2048]{1,0:T(8,128)(2,1)S(1)}, u32[]{:S(2)}, u32[]{:S(2)}) collective-permute-start(bf16[72,2048]{1,0:T(8,128)(2,1)S(1)} %pack.1.refs_0_), channel_id=1, source_target_pairs={{0,128},{128,4},{4,132},{132,0},{1,129},{129,5},{5,133},{133,1},{2... | collective-permute-start | bytes 884744 | tf_op jit(solution)/shard_map/ppermute | solution.py:298
  80.8 10.8 %collective-permute-start.2 = (bf16[40,2048]{1,0:T(8,128)(2,1)S(1)}, bf16[40,2048]{1,0:T(8,128)(2,1)S(1)}, u32[]{:S(2)}, u32[]{:S(2)}) collective-permute-start(bf16[40,2048]{1,0:T(8,128)(2,1)S(1)} %slice.8), channel_id=1, source_target_pairs={{0,128},{128,4},{4,132},{132,0},{1,129},{129,5},{5,133},{133,1},{2... | collective-permute-start | bytes 491528 | tf_op jit(solution)/shard_map/ppermute | solution.py:325
  84.0 6.9 %collective-permute-start.3 = (bf16[32,2048]{1,0:T(8,128)(2,1)S(1)}, bf16[32,2048]{1,0:T(8,128)(2,1)S(1)}, u32[]{:S(2)}, u32[]{:S(2)}) collective-permute-start(bf16[32,2048]{1,0:T(8,128)(2,1)S(1)} %slice.9), channel_id=1, source_target_pairs={{128,0},{4,128},{132,4},{0,132},{129,1},{5,129},{133,5},{1,133},{1... | collective-permute-start | bytes 393224 | tf_op jit(solution)/shard_map/ppermute | solution.py:326
  89.0 48.4 %collective-permute-start.5 = (bf16[2,256,768]{2,1,0:T(8,128)(2,1)}, bf16[2,256,768]{2,1,0:T(8,128)(2,1)}, u32[]{:S(2)}, u32[]{:S(2)}) collective-permute-start(bf16[2,256,768]{2,1,0:T(8,128)(2,1)} %get-tuple-element.27.refs_0_), channel_id=1, source_target_pairs={{0,64},{64,0},{1,65},{65,1},{2,66},{66,2},{3,67},{67,3},{4,68},{68... | collective-permute-start | bytes 2359304 | tf_op jit(solution)/shard_map/ppermute | solution.py:317
  89.0 48.4 %collective-permute-start.6 = (bf16[2,256,768]{2,1,0:T(8,128)(2,1)}, bf16[2,256,768]{2,1,0:T(8,128)(2,1)}, u32[]{:S(2)}, u32[]{:S(2)}) collective-permute-start(bf16[2,256,768]{2,1,0:T(8,128)(2,1)} %collective-permute-done.4.refs_1_), channel_id=1, source_target_pairs={{0,64},{64,0},{1,65},{65,1},{2,66},{66,2},{3,67},{67,3},{4,68},{68... | collective-permute-start | bytes 2359304 | tf_op jit(solution)/shard_map/ppermute | solution.py:318
  92.9 1.2 copy-start
  94.1 61.6 %all-to-all-start = ((bf16[16,24,2048]{2,1,0:T(8,128)(2,1)}), bf16[16,24,2048]{2,1,0:T(8,128)(2,1)S(1)}, u32[]{:S(2)}, u32[]{:S(2)}) async-start(bf16[16,24,2048]{2,1,0:T(8,128)(2,1)} %copy-done), calls=%async_computation | async-start | bytes 3145728 | tf_op jit(solution)/shard_map/all_to_all | solution.py:269
  100.8 31.3 %collective-permute-start.11 = (bf16[768,256]{1,0:T(8,128)(2,1)}, bf16[768,256]{1,0:T(8,128)(2,1)}, u32[]{:S(2)}, u32[]{:S(2)}) collective-permute-start(bf16[768,256]{1,0:T(8,128)(2,1)} %get-tuple-element.31), channel_id=1, source_target_pairs={{0,128},{128,0},{1,129},{129,1},{2,130},{130,2},{3,131},{131,3},{4... | collective-permute-start | bytes 1179656 | tf_op jit(solution)/shard_map/ppermute | solution.py:316
  103.3 40.1 %collective-permute-start.7 = (bf16[2,256,768]{2,1,0:T(8,128)(2,1)}, bf16[2,256,768]{2,1,0:T(8,128)(2,1)}, u32[]{:S(2)}, u32[]{:S(2)}) collective-permute-start(bf16[2,256,768]{2,1,0:T(8,128)(2,1)} %get-tuple-element.27.refs_0_), channel_id=1, source_target_pairs={{0,32},{32,0},{1,33},{33,1},{2,34},{34,2},{3,35},{35,3},{4,36},{36... | collective-permute-start | bytes 2359304 | tf_op jit(solution)/shard_map/ppermute | solution.py:319
  109.1 34.2 %collective-permute-start.12 = (bf16[768,256]{1,0:T(8,128)(2,1)}, bf16[768,256]{1,0:T(8,128)(2,1)}, u32[]{:S(2)}, u32[]{:S(2)}) collective-permute-start(bf16[768,256]{1,0:T(8,128)(2,1)} %get-tuple-element.30.refs_1_.refs_2_), channel_id=1, source_target_pairs={{0,64},{64,0},{1,65},{65,1},{2,66},{66,2},{3,67},{67,3},{4,68},{68... | collective-permute-start | bytes 1179656 | tf_op jit(solution)/shard_map/ppermute | solution.py:317
  132.0 23.1 %collective-permute-start.8 = (bf16[2,256,768]{2,1,0:T(8,128)(2,1)}, bf16[2,256,768]{2,1,0:T(8,128)(2,1)}, u32[]{:S(2)}, u32[]{:S(2)}) collective-permute-start(bf16[2,256,768]{2,1,0:T(8,128)(2,1)} %collective-permute-done.4.refs_1_), channel_id=1, source_target_pairs={{0,32},{32,0},{1,33},{33,1},{2,34},{34,2},{3,35},{35,3},{4,36},{36... | collective-permute-start | bytes 2359304 | tf_op jit(solution)/shard_map/ppermute | solution.py:319
  137.4 17.7 %collective-permute-start.9 = (bf16[2,256,768]{2,1,0:T(8,128)(2,1)}, bf16[2,256,768]{2,1,0:T(8,128)(2,1)}, u32[]{:S(2)}, u32[]{:S(2)}) collective-permute-start(bf16[2,256,768]{2,1,0:T(8,128)(2,1)} %collective-permute-done.5.refs_2_), channel_id=1, source_target_pairs={{0,32},{32,0},{1,33},{33,1},{2,34},{34,2},{3,35},{35,3},{4,36},{36... | collective-permute-start | bytes 2359304 | tf_op jit(solution)/shard_map/ppermute | solution.py:319
  137.4 18.2 %collective-permute-start.10 = (bf16[2,256,768]{2,1,0:T(8,128)(2,1)}, bf16[2,256,768]{2,1,0:T(8,128)(2,1)}, u32[]{:S(2)}, u32[]{:S(2)}) collective-permute-start(bf16[2,256,768]{2,1,0:T(8,128)(2,1)} %collective-permute-done.6.refs_3_), channel_id=1, source_target_pairs={{0,32},{32,0},{1,33},{33,1},{2,34},{34,2},{3,35},{35,3},{4,36},{36... | collective-permute-start | bytes 2359304 | tf_op jit(solution)/shard_map/ppermute | solution.py:319
  143.3 9.6 %collective-permute-start.13 = (bf16[768,256]{1,0:T(8,128)(2,1)}, bf16[768,256]{1,0:T(8,128)(2,1)}, u32[]{:S(2)}, u32[]{:S(2)}) collective-permute-start(bf16[768,256]{1,0:T(8,128)(2,1)} %collective-permute-done.11.refs_2_.refs_3_), channel_id=1, source_target_pairs={{0,64},{64,0},{1,65},{65,1},{2,66},{66,2},{3,67},{67,3},{4,68},{68... | collective-permute-start | bytes 1179656 | tf_op jit(solution)/shard_map/ppermute | solution.py:318
  143.4 21.3 %copy-start.11 = (s32[8]{0:T(128)}, s32[8]{0:T(128)S(1)}, u32[]{:S(2)}) copy-start(s32[8]{0:T(128)S(1)} %stack.47.off_ref) | copy-start | bytes 100
  143.4 23.5 %collective-permute-start.14 = (bf16[768,256]{1,0:T(8,128)(2,1)}, bf16[768,256]{1,0:T(8,128)(2,1)}, u32[]{:S(2)}, u32[]{:S(2)}) collective-permute-start(bf16[768,256]{1,0:T(8,128)(2,1)} %get-tuple-element.30.refs_1_.refs_2_), channel_id=1, source_target_pairs={{0,32},{32,0},{1,33},{33,1},{2,34},{34,2},{3,35},{35,3},{4,36},{36... | collective-permute-start | bytes 1179656 | tf_op jit(solution)/shard_map/ppermute | solution.py:319
  152.9 14.0 %collective-permute-start.15 = (bf16[768,256]{1,0:T(8,128)(2,1)}, bf16[768,256]{1,0:T(8,128)(2,1)}, u32[]{:S(2)}, u32[]{:S(2)}) collective-permute-start(bf16[768,256]{1,0:T(8,128)(2,1)} %collective-permute-done.11.refs_2_.refs_3_), channel_id=1, source_target_pairs={{0,32},{32,0},{1,33},{33,1},{2,34},{34,2},{3,35},{35,3},{4,36},{36... | collective-permute-start | bytes 1179656 | tf_op jit(solution)/shard_map/ppermute | solution.py:319
  155.1 11.8 %collective-permute-start.16 = (bf16[768,256]{1,0:T(8,128)(2,1)}, bf16[768,256]{1,0:T(8,128)(2,1)}, u32[]{:S(2)}, u32[]{:S(2)}) collective-permute-start(bf16[768,256]{1,0:T(8,128)(2,1)} %collective-permute-done.12.refs_3_.refs_4_), channel_id=1, source_target_pairs={{0,32},{32,0},{1,33},{33,1},{2,34},{34,2},{3,35},{35,3},{4,36},{36... | collective-permute-start | bytes 1179656 | tf_op jit(solution)/shard_map/ppermute | solution.py:319
  155.2 11.8 %collective-permute-start.17 = (bf16[768,256]{1,0:T(8,128)(2,1)}, bf16[768,256]{1,0:T(8,128)(2,1)}, u32[]{:S(2)}, u32[]{:S(2)}) collective-permute-start(bf16[768,256]{1,0:T(8,128)(2,1)} %collective-permute-done.13.refs_4_.refs_5_), channel_id=1, source_target_pairs={{0,32},{32,0},{1,33},{33,1},{2,34},{34,2},{3,35},{35,3},{4,36},{36... | collective-permute-start | bytes 1179656 | tf_op jit(solution)/shard_map/ppermute | solution.py:319
  173.5 40.4 %all-to-all-start.3 = ((bf16[16,40,2048]{2,1,0:T(8,128)(2,1)}), bf16[16,40,2048]{2,1,0:T(8,128)(2,1)S(1)}, u32[]{:S(2)}, u32[]{:S(2)}) async-start(bf16[16,40,2048]{2,1,0:T(8,128)(2,1)} %shard_map.85), calls=%async_computation.3 | async-start | bytes 5242880 | tf_op jit(solution)/shard_map/all_to_all | solution.py:269
  213.9 29.8 %all-to-all-start.2 = ((bf16[16,8,2048]{2,1,0:T(8,128)(2,1)}), bf16[16,8,2048]{2,1,0:T(8,128)(2,1)S(1)}, u32[]{:S(2)}, u32[]{:S(2)}) async-start(bf16[16,8,2048]{2,1,0:T(8,128)(2,1)} %shard_map.84), calls=%async_computation.2 | async-start | bytes 1048576 | tf_op jit(solution)/shard_map/all_to_all | solution.py:269
  226.9 16.8 %copy-start.2 = (f32[64,2048]{1,0:T(8,128)S(1)}, f32[64,2048]{1,0:T(8,128)}, u32[]{:S(2)}) copy-start(f32[64,2048]{1,0:T(8,128)} %copy-done.1) | copy-start | bytes 1572868
  226.9 8.4 %collective-permute-start.20 = (bf16[32,2048]{1,0:T(8,128)(2,1)S(1)}, bf16[32,2048]{1,0:T(8,128)(2,1)S(1)}, u32[]{:S(2)}, u32[]{:S(2)}) collective-permute-start(bf16[32,2048]{1,0:T(8,128)(2,1)S(1)} %get-tuple-element.42), channel_id=1, source_target_pairs={{0,128},{128,4},{4,132},{132,0},{1,129},{129,5},{5,133},{133,1},{2... | collective-permute-start | bytes 393224 | tf_op jit(solution)/shard_map/ppermute | solution.py:400
  226.9 10.8 %collective-permute-start.18 = (bf16[32,2048]{1,0:T(8,128)(2,1)S(1)}, bf16[32,2048]{1,0:T(8,128)(2,1)S(1)}, u32[]{:S(2)}, u32[]{:S(2)}) collective-permute-start(bf16[32,2048]{1,0:T(8,128)(2,1)S(1)} %get-tuple-element.39), channel_id=1, source_target_pairs={{128,0},{4,128},{132,4},{0,132},{129,1},{5,129},{133,5},{1,133},{1... | collective-permute-start | bytes 393224 | tf_op jit(solution)/shard_map/ppermute | solution.py:399
  237.7 10.3 %collective-permute-start.21 = (bf16[64,2048]{1,0:T(8,128)(2,1)}, bf16[64,2048]{1,0:T(8,128)(2,1)S(1)}, u32[]{:S(2)}, u32[]{:S(2)}) collective-permute-start(bf16[64,2048]{1,0:T(8,128)(2,1)} %shard_map.89), channel_id=1, source_target_pairs={{0,128},{128,4},{4,132},{132,0},{1,129},{129,5},{5,133},{133,1},{2... | collective-permute-start | bytes 786440 | tf_op jit(solution)/shard_map/ppermute | solution.py:405
  240.1 13.7 %collective-permute-start.19 = (bf16[64,2048]{1,0:T(8,128)(2,1)}, bf16[64,2048]{1,0:T(8,128)(2,1)S(1)}, u32[]{:S(2)}, u32[]{:S(2)}) collective-permute-start(bf16[64,2048]{1,0:T(8,128)(2,1)} %shard_map.88), channel_id=1, source_target_pairs={{128,0},{4,128},{132,4},{0,132},{129,1},{5,129},{133,5},{1,133},{1... | collective-permute-start | bytes 786440 | tf_op jit(solution)/shard_map/ppermute | solution.py:403
  (15 other events, 11.1 us)
